TPU v7x, 32 devices: a whole 2x2x4 slice. The times are simulated.
32 devices in a mesh: seq: 8 (over z, x), head: 4 (over y, core).
Axes of the slice: x: 2, y: 2, z: 4, core: 2. Of those that a mesh axis runs over, the one named last changes fastest.
Arguments:
- block_order: int32 [16], replicated, may hold values from 0 to 15, each once
- queries: bfloat16 [2048, 4096], P('seq', 'head'), may hold values from -52 to 52
- keys: bfloat16 [2048, 4096], P('seq', 'head'), may hold values from -4.5 to 4.5
- values: bfloat16 [2048, 4096], P('seq', 'head'), may hold values from -5 to 5
- hyena_q: bfloat16 [2048, 4096], P('seq', 'head'), may hold values from -5 to 5
- hyena_k: bfloat16 [2048, 4096], P('seq', 'head'), may hold values from -5 to 5
- hyena_v: bfloat16 [2048, 4096], P('seq', 'head'), may hold values from -5 to 5
- hyena_grad: bfloat16 [2048, 4096], P('seq', 'head'), may hold values from -5 to 5
- filters: float32 [256, 128], P('head'), may hold values from -0.5 to 0.5
- proj_weight: bfloat16 [3, 4096, 4096], P(None, None, 'head'), may hold values from -0.0546875 to 0.0546875
Outputs:
- input_grad: bfloat16 [2048, 4096], P('seq', 'head')
- query_grad: bfloat16 [2048, 4096], P('seq', 'head')
- key_grad: bfloat16 [2048, 4096], P('seq', 'head')
- value_grad: bfloat16 [2048, 4096], P('seq', 'head')
Inputs may be any that keep to these rules, and one draw needn't show every extreme that they name: `block_order`: A permutation of the sequence blocks; entry 2 d + j is the position block of rows d * 256 + j * 128 to d * 256 + j * 128 + 127.
All inputs are finite; a program needn't handle non-finite values.
Results may differ from a plain program's by a relative error of at most 0.01.
Values may be sent and summed in bfloat16 or wider, within the bound.
A program may use at most 128 MiB of HBM per device.

v0:
```python
import jax
import jax.numpy as jnp
from jax import lax
from jax.sharding import PartitionSpec as P

HD = 128
GROUP = 16
KL = 128
BLOCK = 128


def for_sending(x):

    def short(part):
        return part.astype(jnp.bfloat16) if part.dtype == jnp.float32 else part

    return jax.tree.map(short, x)


def passed_along(value, axis, steps):
    count = lax.axis_size(axis)
    pairs = [(source, (source + steps) % count) for source in range(count)]
    return lax.ppermute(value, axis, pairs)


def keep_state(current):
    return current


def per_device(
    block_order, queries, keys, values, hyena_q, hyena_k, hyena_v, hyena_grad, filters, proj_weight
):
    seq_count = lax.axis_size("seq")
    my_index = lax.axis_index("seq")
    row_count = queries.shape[0]
    feature_width = queries.shape[1]
    head_count = feature_width // HD
    block_total = block_order.shape[0]
    offsets = jnp.arange(BLOCK, dtype=jnp.int32)
    block_ids = jnp.arange(block_total, dtype=jnp.int32)

    def block_positions(source):
        block_pair = lax.dynamic_slice_in_dim(block_order, 2 * source, 2)
        return jnp.concatenate([block_pair[0] * BLOCK + offsets, block_pair[1] * BLOCK + offsets])

    def holder_of(target):
        return jnp.sum(jnp.where(block_order == target, block_ids, 0))

    my_positions = block_positions(my_index)
    product_kv = (hyena_k.astype(jnp.float32) * hyena_v.astype(jnp.float32)).astype(jnp.bfloat16)
    product_dq = (hyena_grad.astype(jnp.float32) * hyena_q.astype(jnp.float32)).astype(jnp.bfloat16)
    my_blocks = [
        lax.dynamic_index_in_dim(block_order, 2 * my_index + portion, 0, keepdims=False)
        for portion in range(2)
    ]
    gathered_z, gathered_dc = (
        lax.all_gather(product_kv, "seq", axis=0, tiled=True),
        lax.all_gather(product_dq, "seq", axis=0, tiled=True),
    )
    group_count = filters.shape[0]
    channels = hyena_q.shape[1]
    out_rows = jnp.arange(BLOCK)[:, None, None]
    window_rows = jnp.arange(BLOCK + KL)[None, :, None]
    tap_ids = jnp.arange(KL)[None, None, :]
    causal_table = (out_rows + KL - window_rows == tap_ids).astype(jnp.float32)
    anti_table = (window_rows - out_rows == tap_ids).astype(jnp.float32)
    causal_toeplitz = jnp.einsum(
        "gj,tsj->gts", filters, causal_table, precision=lax.Precision.HIGHEST
    )
    anti_toeplitz = jnp.einsum("gj,tsj->gts", filters, anti_table, precision=lax.Precision.HIGHEST)

    def apply_groups(toeplitz, window):
        grouped = window.astype(jnp.float32).reshape(BLOCK + KL, group_count, GROUP)
        result = jnp.einsum("gts,sgk->tgk", toeplitz, grouped, precision=lax.Precision.HIGHEST)
        return result.reshape(BLOCK, channels)

    conv_parts = []
    back_parts = []
    for portion in range(2):
        block_id = my_blocks[portion]
        before = lax.dynamic_slice_in_dim(
            gathered_z, holder_of(block_id - 1) * BLOCK + BLOCK - KL, KL, 0
        )
        before = jnp.where(block_id >= 1, before, jnp.zeros_like(before))
        after = lax.dynamic_slice_in_dim(gathered_dc, holder_of(block_id + 1) * BLOCK, KL, 0)
        after = jnp.where(block_id + 1 < block_total, after, jnp.zeros_like(after))
        own_z = product_kv[portion * BLOCK : (portion + 1) * BLOCK]
        own_dc = product_dq[portion * BLOCK : (portion + 1) * BLOCK]
        conv_parts.append(apply_groups(causal_toeplitz, jnp.concatenate([before, own_z])))
        back_parts.append(apply_groups(anti_toeplitz, jnp.concatenate([own_dc, after])))
    convolved = jnp.concatenate(conv_parts)
    back_conv = jnp.concatenate(back_parts)
    stacked = jnp.stack(
        [
            hyena_grad.astype(jnp.float32) * convolved,
            back_conv * hyena_v.astype(jnp.float32),
            back_conv * hyena_k.astype(jnp.float32),
        ]
    ).astype(jnp.bfloat16)
    summed = lax.psum_scatter(
        jnp.einsum("mic,mtc->it", proj_weight, stacked, preferred_element_type=jnp.float32),
        "head",
        scatter_dimension=0,
        tiled=True,
    )
    input_grad = summed.T.astype(jnp.bfloat16)
    score_scale = HD ** (-0.5)
    query_heads = queries.reshape(row_count, head_count, HD)
    key_heads = keys.reshape(row_count, head_count, HD)
    value_heads = values.reshape(row_count, head_count, HD)
    grad_heads = input_grad.reshape(row_count, head_count, HD)

    def tile_scores(query_block, key_block, query_pos, key_pos):
        scores = (
            jnp.einsum("qhd,khd->hqk", query_block, key_block, preferred_element_type=jnp.float32)
            * score_scale
        )
        allowed = (key_pos[None, :] <= query_pos[:, None])[None]
        return (scores, allowed)

    def stat_update(running, key_block, value_block, source):
        key_pos = block_positions(source)
        active = jnp.min(key_pos) <= jnp.max(my_positions)

        def stat_accumulate(current):
            row_max, row_sum, row_dot = current
            scores, allowed = tile_scores(query_heads, key_block, my_positions, key_pos)
            masked = jnp.where(allowed, scores, -1e30)
            new_max = jnp.maximum(row_max, jnp.max(masked, axis=2))
            terms = jnp.where(allowed, jnp.exp(masked - new_max[:, :, None]), 0.0)
            prob_grad = jnp.einsum(
                "qhd,khd->hqk", grad_heads, value_block, preferred_element_type=jnp.float32
            )
            factor = jnp.exp(row_max - new_max)
            return (
                new_max,
                row_sum * factor + jnp.sum(terms, axis=2),
                row_dot * factor + jnp.sum(terms * prob_grad, axis=2),
            )

        return lax.cond(active, stat_accumulate, keep_state, running)

    initial = (
        jnp.full((head_count, row_count), -1e30, jnp.float32),
        jnp.zeros((head_count, row_count), jnp.float32),
        jnp.zeros((head_count, row_count), jnp.float32),
    )

    def tile_grads(
        query_block, grad_block, norm_block, delta_block, query_pos, key_block, value_block, key_pos
    ):
        scores, allowed = tile_scores(query_block, key_block, query_pos, key_pos)
        probabilities = jnp.where(allowed, jnp.exp(scores - norm_block[:, :, None]), 0.0)
        prob_grad = jnp.einsum(
            "qhd,khd->hqk", grad_block, value_block, preferred_element_type=jnp.float32
        )
        score_grad = probabilities * (prob_grad - delta_block[:, :, None])
        probs_low = probabilities.astype(jnp.bfloat16)
        score_low = score_grad.astype(jnp.bfloat16)
        add_query = (
            jnp.einsum("hqk,khd->qhd", score_low, key_block, preferred_element_type=jnp.float32)
            * score_scale
        )
        add_key = (
            jnp.einsum("hqk,qhd->khd", score_low, query_block, preferred_element_type=jnp.float32)
            * score_scale
        )
        add_value = jnp.einsum(
            "hqk,qhd->khd", probs_low, grad_block, preferred_element_type=jnp.float32
        )
        return (add_query, add_key, add_value)

    zero_rows = jnp.zeros((row_count, head_count, HD), jnp.float32)

    def move_stat_queries(pair):
        return jax.tree.map(
            lambda part, own: part.astype(own.dtype),
            passed_along(for_sending(pair), "seq", 1),
            pair,
        )

    def stat_turn(turn_index, loop_state):
        running, key_block, value_block = loop_state
        source = (my_index - turn_index) % seq_count
        running = stat_update(running, key_block, value_block, source)
        key_block, value_block = move_stat_queries((key_block, value_block))
        return (running, key_block, value_block)

    loop_state = lax.fori_loop(0, seq_count - 1, stat_turn, (initial, key_heads, value_heads))
    running = stat_update(
        loop_state[0], loop_state[1], loop_state[2], (my_index - (seq_count - 1)) % seq_count
    )
    log_norm = running[0] + jnp.log(running[1])
    row_delta = running[2] / running[1]

    def query_turn(turn_index, loop_state):
        query_block, grad_block, norm_block, delta_block, query_acc, key_acc, value_acc = loop_state
        source = (my_index - turn_index) % seq_count
        query_pos = block_positions(source)
        active = jnp.min(my_positions) <= jnp.max(query_pos)

        def query_accumulate(current):
            add_query, add_key, add_value = tile_grads(
                query_block,
                grad_block,
                norm_block,
                delta_block,
                query_pos,
                key_heads,
                value_heads,
                my_positions,
            )
            return (current[0] + add_query, current[1] + add_key, current[2] + add_value)

        query_acc, key_acc, value_acc = lax.cond(
            active, query_accumulate, keep_state, (query_acc, key_acc, value_acc)
        )
        query_block, grad_block = passed_along((query_block, grad_block), "seq", 1)
        norm_block, delta_block, query_acc = passed_along(
            (norm_block, delta_block, query_acc), "seq", 1
        )
        return (query_block, grad_block, norm_block, delta_block, query_acc, key_acc, value_acc)

    final_state = lax.fori_loop(
        0,
        seq_count,
        query_turn,
        (query_heads, grad_heads, log_norm, row_delta, zero_rows, zero_rows, zero_rows),
    )
    query_total = final_state[4]
    key_total = final_state[5]
    value_total = final_state[6]
    query_grad = query_total.reshape(row_count, feature_width).astype(jnp.bfloat16)
    key_grad = key_total.reshape(row_count, feature_width).astype(jnp.bfloat16)
    value_grad = value_total.reshape(row_count, feature_width).astype(jnp.bfloat16)
    return (input_grad, query_grad, key_grad, value_grad)


def solution(mesh):
    placed = (
        P(),
        P("seq", "head"),
        P("seq", "head"),
        P("seq", "head"),
        P("seq", "head"),
        P("seq", "head"),
        P("seq", "head"),
        P("seq", "head"),
        P("head", None),
        P(None, None, "head"),
    )
    return jax.shard_map(
        per_device,
        mesh=mesh,
        in_specs=placed,
        out_specs=(P("seq", "head"), P("seq", "head"), P("seq", "head"), P("seq", "head")),
        check_vma=False,
    )
```

profile of v0, /device:TPU:0, one launch (start us, length us, event | category | flops | bytes accessed | tf_op | source)
XLA Modules:
  0.0 889.9 jit_solution(11407967144494045220)
XLA Ops:
  15.8 15.1 %fusion.31 = f32[64,128,256]{2,0,1:T(8,128)} fusion(s32[128,256]{1,0:T(8,128)S(1)} %iota_subtract_fusion, f32[64,128]{1,0:T(8,128)S(1)} %copy-done), kind=kOutput, calls=%fused_computation.58 | convolution fusion | flops 3225419776 | bytes 8552448 | tf_op jit(solution)/shard_map/gj,tsj->gts/dot_general | solution.py:70
  30.9 55.4 %all-gather.5.cloned.1.call-done = bf16[2048,1024]{1,0:T(8,128)(2,1)} async-done(((bf16[256,1024]{1,0:T(8,128)(2,1)}), bf16[2048,1024]{1,0:T(8,128)(2,1)}) %all-gather.5.cloned.1.call-update) | async-done | bytes 4194320 | tf_op jit(solution)/shard_map/all_gather | solution.py:58
  87.7 11.7 %fusion.25 = f32[64,16,128]{2,1,0:T(8,128)S(1)} fusion(bf16[256,64,16]{0,2,1:T(8,128)(2,1)S(1)} %bitcast.124, f32[64,128,256]{2,0,1:T(8,128)} %fusion.31), kind=kOutput, calls=%fused_computation.51 | convolution fusion | flops 402653184 | bytes 9437184 | tf_op jit(solution)/shard_map/gts,sgk->tgk/dot_general | solution.py:74
  99.8 11.7 %fusion.23 = f32[64,16,128]{2,1,0:T(8,128)S(1)} fusion(bf16[256,64,16]{0,2,1:T(8,128)(2,1)S(1)} %bitcast.120, f32[64,128,256]{2,0,1:T(8,128)} %fusion.31), kind=kOutput, calls=%fused_computation.49 | convolution fusion | flops 402653184 | bytes 9437184 | tf_op jit(solution)/shard_map/gts,sgk->tgk/dot_general | solution.py:74
  116.2 15.1 %fusion.32 = f32[64,128,256]{2,0,1:T(8,128)} fusion(s32[128,256]{1,0:T(8,128)S(1)} %iota_subtract_fusion.1, f32[64,128]{1,0:T(8,128)S(1)} %copy-done), kind=kOutput, calls=%fused_computation.59 | convolution fusion | flops 3225419776 | bytes 8552448 | tf_op jit(solution)/shard_map/gj,tsj->gts/dot_general | solution.py:67
  131.4 53.4 %all-gather.3.cloned.1.call-done = bf16[2048,1024]{1,0:T(8,128)(2,1)} async-done(((bf16[256,1024]{1,0:T(8,128)(2,1)}), bf16[2048,1024]{1,0:T(8,128)(2,1)}) %all-gather.3.cloned.1.call-update) | async-done | bytes 4194320 | tf_op jit(solution)/shard_map/all_gather | solution.py:57
  186.2 11.7 %fusion.29 = f32[64,16,128]{2,1,0:T(8,128)S(1)} fusion(bf16[256,64,16]{0,2,1:T(8,128)(2,1)S(1)} %bitcast.126, f32[64,128,256]{2,0,1:T(8,128)} %fusion.32), kind=kOutput, calls=%fused_computation.55 | convolution fusion | flops 402653184 | bytes 9437184 | tf_op jit(solution)/shard_map/gts,sgk->tgk/dot_general | solution.py:74
  198.3 11.7 %fusion.27 = f32[64,16,128]{2,1,0:T(8,128)S(1)} fusion(bf16[256,64,16]{0,2,1:T(8,128)(2,1)S(1)} %bitcast.122, f32[64,128,256]{2,0,1:T(8,128)} %fusion.32), kind=kOutput, calls=%fused_computation.53 | convolution fusion | flops 402653184 | bytes 9437184 | tf_op jit(solution)/shard_map/gts,sgk->tgk/dot_general | solution.py:74
  211.2 14.0 %convolution_bitcast_fusion.1 = f32[4096,256]{0,1:T(8,128)} fusion(bf16[3,4096,1024]{2,1,0:T(8,128)(2,1)} %param.29, bf16[1,256,1024]{2,1,0:T(8,128)(2,1)S(1)} %copy-done.17, bf16[1,256,1024]{2,1,0:T(8,128)(2,1)S(1)} %copy-done.16, bf16[1,256,1024]{2,1,0:T(8,128)(2,1)S(1)} %fusion.45), kind=kOutput, calls=%fused_computation.57 | convolution fusion | flops 6444023808 | bytes 30932992 | tf_op jit(solution)/shard_map/mic,mtc->it/dot_general | solution.py:101
  237.9 30.4 %reduce-scatter.2.cloned.1.call-done = f32[1024,256]{0,1:T(8,128)} async-done(((f32[4096,256]{0,1:T(8,128)}), f32[1024,256]{0,1:T(8,128)}) %reduce-scatter.2.cloned.1.call-update) | async-done | bytes 1048592 | tf_op jit(solution)/shard_map/reduce_scatter | solution.py:100
  271.8 181.1 %while.54 = (s32[]{:T(128)}, f32[8,256]{1,0:T(8,128)S(1)}, f32[8,256]{1,0:T(8,128)S(1)}, f32[8,256]{1,0:T(8,128)S(1)}, bf16[256,8,128]{2,0,1:T(8,128)(2,1)S(1)},...) while((s32[]{:T(128)}, f32[8,256]{1,0:T(8,128)S(1)}, ...), condition=%wide.region_17.18_spmd.clone.clone, body=%wide.region_9.17_spmd.clone.clone.sunk | while | flops 275848224 | bytes 15095442 | solution.py:189
  290.3 9.9 %collective-permute-done.1 = bf16[256,8,128]{2,0,1:T(8,128)(2,1)S(1)} collective-permute-done((bf16[256,8,128]{2,0,1:T(8,128)(2,1)}, bf16[256,8,128]{2,0,1:T(8,128)(2,1)S(1)}, u32[]{:S(2)}, u32[]{:S(2)}) %collective-permute-start.1) | collective-permute-done | bytes 524320 | tf_op jit(solution)/shard_map/while/body/eval_jaxpr/ppermute | solution.py:23
  318.7 9.1 %collective-permute-done.1 = bf16[256,8,128]{2,0,1:T(8,128)(2,1)S(1)} collective-permute-done((bf16[256,8,128]{2,0,1:T(8,128)(2,1)}, bf16[256,8,128]{2,0,1:T(8,128)(2,1)S(1)}, u32[]{:S(2)}, u32[]{:S(2)}) %collective-permute-start.1) | collective-permute-done | bytes 524320 | tf_op jit(solution)/shard_map/while/body/eval_jaxpr/ppermute | solution.py:23
  337.6 8.7 collective-permute-done
  364.3 8.8 collective-permute-done
  457.1 421.9 %while.55 = (s32[]{:T(128)}, bf16[256,8,128]{2,0,1:T(8,128)(2,1)S(1)}, bf16[256,8,128]{2,0,1:T(8,128)(2,1)}, f32[8,256]{1,0:T(8,128)S(1)}, f32[8,256]{1,0:T(8,12...) while((s32[]{:T(128)}, ...), condition=%wide.region_30.31_spmd.clone.clone, body=%wide.region_25.30_spmd.clone.clone.sunk | while | flops 676135936 | bytes 51107764 | solution.py:224
  468.9 28.7 %collective-permute-done.6 = f32[256,8,128]{2,0,1:T(8,128)} collective-permute-done((f32[256,8,128]{2,0,1:T(8,128)S(1)}, f32[256,8,128]{2,0,1:T(8,128)}, u32[]{:S(2)}, u32[]{:S(2)}) %collective-permute-start.6) | collective-permute-done | bytes 1048608 | tf_op jit(solution)/shard_map/while/body/eval_jaxpr/ppermute | solution.py:23
  498.8 14.1 %collective-permute-done.4 = f32[8,256]{1,0:T(8,128)S(1)} collective-permute-done((f32[8,256]{1,0:T(8,128)S(1)}, f32[8,256]{1,0:T(8,128)S(1)}, u32[]{:S(2)}, u32[]{:S(2)}) %collective-permute-start.4) | collective-permute-done | bytes 8224 | tf_op jit(solution)/shard_map/while/body/eval_jaxpr/ppermute | solution.py:23
  524.6 28.7 %collective-permute-done.6 = f32[256,8,128]{2,0,1:T(8,128)} collective-permute-done((f32[256,8,128]{2,0,1:T(8,128)S(1)}, f32[256,8,128]{2,0,1:T(8,128)}, u32[]{:S(2)}, u32[]{:S(2)}) %collective-permute-start.6) | collective-permute-done | bytes 1048608 | tf_op jit(solution)/shard_map/while/body/eval_jaxpr/ppermute | solution.py:23
  554.5 13.3 %collective-permute-done.4 = f32[8,256]{1,0:T(8,128)S(1)} collective-permute-done((f32[8,256]{1,0:T(8,128)S(1)}, f32[8,256]{1,0:T(8,128)S(1)}, u32[]{:S(2)}, u32[]{:S(2)}) %collective-permute-start.4) | collective-permute-done | bytes 8224 | tf_op jit(solution)/shard_map/while/body/eval_jaxpr/ppermute | solution.py:23
  579.4 28.7 %collective-permute-done.6 = f32[256,8,128]{2,0,1:T(8,128)} collective-permute-done((f32[256,8,128]{2,0,1:T(8,128)S(1)}, f32[256,8,128]{2,0,1:T(8,128)}, u32[]{:S(2)}, u32[]{:S(2)}) %collective-permute-start.6) | collective-permute-done | bytes 1048608 | tf_op jit(solution)/shard_map/while/body/eval_jaxpr/ppermute | solution.py:23
  609.3 12.4 %collective-permute-done.4 = f32[8,256]{1,0:T(8,128)S(1)} collective-permute-done((f32[8,256]{1,0:T(8,128)S(1)}, f32[8,256]{1,0:T(8,128)S(1)}, u32[]{:S(2)}, u32[]{:S(2)}) %collective-permute-start.4) | collective-permute-done | bytes 8224 | tf_op jit(solution)/shard_map/while/body/eval_jaxpr/ppermute | solution.py:23
  633.3 28.7 %collective-permute-done.6 = f32[256,8,128]{2,0,1:T(8,128)} collective-permute-done((f32[256,8,128]{2,0,1:T(8,128)S(1)}, f32[256,8,128]{2,0,1:T(8,128)}, u32[]{:S(2)}, u32[]{:S(2)}) %collective-permute-start.6) | collective-permute-done | bytes 1048608 | tf_op jit(solution)/shard_map/while/body/eval_jaxpr/ppermute | solution.py:23
  663.3 11.6 %collective-permute-done.4 = f32[8,256]{1,0:T(8,128)S(1)} collective-permute-done((f32[8,256]{1,0:T(8,128)S(1)}, f32[8,256]{1,0:T(8,128)S(1)}, u32[]{:S(2)}, u32[]{:S(2)}) %collective-permute-start.4) | collective-permute-done | bytes 8224 | tf_op jit(solution)/shard_map/while/body/eval_jaxpr/ppermute | solution.py:23
  686.4 28.7 %collective-permute-done.6 = f32[256,8,128]{2,0,1:T(8,128)} collective-permute-done((f32[256,8,128]{2,0,1:T(8,128)S(1)}, f32[256,8,128]{2,0,1:T(8,128)}, u32[]{:S(2)}, u32[]{:S(2)}) %collective-permute-start.6) | collective-permute-done | bytes 1048608 | tf_op jit(solution)/shard_map/while/body/eval_jaxpr/ppermute | solution.py:23
  716.3 10.7 %collective-permute-done.4 = f32[8,256]{1,0:T(8,128)S(1)} collective-permute-done((f32[8,256]{1,0:T(8,128)S(1)}, f32[8,256]{1,0:T(8,128)S(1)}, u32[]{:S(2)}, u32[]{:S(2)}) %collective-permute-start.4) | collective-permute-done | bytes 8224 | tf_op jit(solution)/shard_map/while/body/eval_jaxpr/ppermute | solution.py:23
  738.7 28.5 %collective-permute-done.6 = f32[256,8,128]{2,0,1:T(8,128)} collective-permute-done((f32[256,8,128]{2,0,1:T(8,128)S(1)}, f32[256,8,128]{2,0,1:T(8,128)}, u32[]{:S(2)}, u32[]{:S(2)}) %collective-permute-start.6) | collective-permute-done | bytes 1048608 | tf_op jit(solution)/shard_map/while/body/eval_jaxpr/ppermute | solution.py:23
  768.4 10.0 %collective-permute-done.4 = f32[8,256]{1,0:T(8,128)S(1)} collective-permute-done((f32[8,256]{1,0:T(8,128)S(1)}, f32[8,256]{1,0:T(8,128)S(1)}, u32[]{:S(2)}, u32[]{:S(2)}) %collective-permute-start.4) | collective-permute-done | bytes 8224 | tf_op jit(solution)/shard_map/while/body/eval_jaxpr/ppermute | solution.py:23
  790.0 27.8 %collective-permute-done.6 = f32[256,8,128]{2,0,1:T(8,128)} collective-permute-done((f32[256,8,128]{2,0,1:T(8,128)S(1)}, f32[256,8,128]{2,0,1:T(8,128)}, u32[]{:S(2)}, u32[]{:S(2)}) %collective-permute-start.6) | collective-permute-done | bytes 1048608 | tf_op jit(solution)/shard_map/while/body/eval_jaxpr/ppermute | solution.py:23
  819.0 10.0 %collective-permute-done.4 = f32[8,256]{1,0:T(8,128)S(1)} collective-permute-done((f32[8,256]{1,0:T(8,128)S(1)}, f32[8,256]{1,0:T(8,128)S(1)}, u32[]{:S(2)}, u32[]{:S(2)}) %collective-permute-start.4) | collective-permute-done | bytes 8224 | tf_op jit(solution)/shard_map/while/body/eval_jaxpr/ppermute | solution.py:23
  840.7 27.0 %collective-permute-done.6 = f32[256,8,128]{2,0,1:T(8,128)} collective-permute-done((f32[256,8,128]{2,0,1:T(8,128)S(1)}, f32[256,8,128]{2,0,1:T(8,128)}, u32[]{:S(2)}, u32[]{:S(2)}) %collective-permute-start.6) | collective-permute-done | bytes 1048608 | tf_op jit(solution)/shard_map/while/body/eval_jaxpr/ppermute | solution.py:23
  868.9 10.0 %collective-permute-done.4 = f32[8,256]{1,0:T(8,128)S(1)} collective-permute-done((f32[8,256]{1,0:T(8,128)S(1)}, f32[8,256]{1,0:T(8,128)S(1)}, u32[]{:S(2)}, u32[]{:S(2)}) %collective-permute-start.4) | collective-permute-done | bytes 8224 | tf_op jit(solution)/shard_map/while/body/eval_jaxpr/ppermute | solution.py:23
  (508 shorter events, 318.8 us)
Async XLA Ops:
  7.2 79.1 %all-gather.5.cloned.1.call-start = ((), (), s32[]{:S(2)}) async-start(), calls=%async_computation.2 | async-start | bytes 4718592 | tf_op jit(solution)/shard_map/all_gather | solution.py:58
  9.5 175.3 %all-gather.3.cloned.1.call-start = ((), (), s32[]{:S(2)}) async-start(), calls=%async_computation.1 | async-start | bytes 4718592 | tf_op jit(solution)/shard_map/all_gather | solution.py:57
  113.3 155.1 %reduce-scatter.2.cloned.1.call-start = ((), (), s32[]{:S(2)}) async-start(), calls=%async_computation.3 | async-start | bytes 5242880 | tf_op jit(solution)/shard_map/reduce_scatter | solution.py:100
  468.8 44.3 %collective-permute-start.2 = (bf16[256,8,128]{2,0,1:T(8,128)(2,1)S(1)}, bf16[256,8,128]{2,0,1:T(8,128)(2,1)S(1)}, u32[]{:S(2)}, u32[]{:S(2)}) collective-permute-start(bf16[256,8,128]{2,0,1:T(8,128)(2,1)S(1)} %copy.132), channel_id=1, source_target_pairs={{0,4},{4,8},{8,12},{12,16},{16,20},{20,24},{24,28},{28,0},{1,5},{5... | collective-permute-start | bytes 1572872 | tf_op jit(solution)/shard_map/while/body/eval_jaxpr/ppermute | solution.py:23
  468.8 44.3 %collective-permute-start.3 = (bf16[256,8,128]{2,0,1:T(8,128)(2,1)S(1)}, bf16[256,8,128]{2,0,1:T(8,128)(2,1)}, u32[]{:S(2)}, u32[]{:S(2)}) collective-permute-start(bf16[256,8,128]{2,0,1:T(8,128)(2,1)S(1)} %copy.133), channel_id=1, source_target_pairs={{0,4},{4,8},{8,12},{12,16},{16,20},{20,24},{24,28},{28,0},{1,5},{5... | collective-permute-start | bytes 1572872 | tf_op jit(solution)/shard_map/while/body/eval_jaxpr/ppermute | solution.py:23
  468.8 44.2 %collective-permute-start.4 = (f32[8,256]{1,0:T(8,128)S(1)}, f32[8,256]{1,0:T(8,128)S(1)}, u32[]{:S(2)}, u32[]{:S(2)}) collective-permute-start(f32[8,256]{1,0:T(8,128)S(1)} %copy.134), channel_id=1, source_target_pairs={{0,4},{4,8},{8,12},{12,16},{16,20},{20,24},{24,28},{28,0},{1,5},{5... | collective-permute-start | bytes 24584 | tf_op jit(solution)/shard_map/while/body/eval_jaxpr/ppermute | solution.py:23
  468.9 44.2 %collective-permute-start.5 = (f32[8,256]{1,0:T(8,128)S(1)}, f32[8,256]{1,0:T(8,128)S(1)}, u32[]{:S(2)}, u32[]{:S(2)}) collective-permute-start(f32[8,256]{1,0:T(8,128)S(1)} %copy.135), channel_id=1, source_target_pairs={{0,4},{4,8},{8,12},{12,16},{16,20},{20,24},{24,28},{28,0},{1,5},{5... | collective-permute-start | bytes 24584 | tf_op jit(solution)/shard_map/while/body/eval_jaxpr/ppermute | solution.py:23
  524.4 43.4 %collective-permute-start.2 = (bf16[256,8,128]{2,0,1:T(8,128)(2,1)S(1)}, bf16[256,8,128]{2,0,1:T(8,128)(2,1)S(1)}, u32[]{:S(2)}, u32[]{:S(2)}) collective-permute-start(bf16[256,8,128]{2,0,1:T(8,128)(2,1)S(1)} %copy.132), channel_id=1, source_target_pairs={{0,4},{4,8},{8,12},{12,16},{16,20},{20,24},{24,28},{28,0},{1,5},{5... | collective-permute-start | bytes 1572872 | tf_op jit(solution)/shard_map/while/body/eval_jaxpr/ppermute | solution.py:23
  524.4 43.4 %collective-permute-start.3 = (bf16[256,8,128]{2,0,1:T(8,128)(2,1)S(1)}, bf16[256,8,128]{2,0,1:T(8,128)(2,1)}, u32[]{:S(2)}, u32[]{:S(2)}) collective-permute-start(bf16[256,8,128]{2,0,1:T(8,128)(2,1)S(1)} %copy.133), channel_id=1, source_target_pairs={{0,4},{4,8},{8,12},{12,16},{16,20},{20,24},{24,28},{28,0},{1,5},{5... | collective-permute-start | bytes 1572872 | tf_op jit(solution)/shard_map/while/body/eval_jaxpr/ppermute | solution.py:23
  524.5 43.3 %collective-permute-start.4 = (f32[8,256]{1,0:T(8,128)S(1)}, f32[8,256]{1,0:T(8,128)S(1)}, u32[]{:S(2)}, u32[]{:S(2)}) collective-permute-start(f32[8,256]{1,0:T(8,128)S(1)} %copy.134), channel_id=1, source_target_pairs={{0,4},{4,8},{8,12},{12,16},{16,20},{20,24},{24,28},{28,0},{1,5},{5... | collective-permute-start | bytes 24584 | tf_op jit(solution)/shard_map/while/body/eval_jaxpr/ppermute | solution.py:23
  524.5 43.3 %collective-permute-start.5 = (f32[8,256]{1,0:T(8,128)S(1)}, f32[8,256]{1,0:T(8,128)S(1)}, u32[]{:S(2)}, u32[]{:S(2)}) collective-permute-start(f32[8,256]{1,0:T(8,128)S(1)} %copy.135), channel_id=1, source_target_pairs={{0,4},{4,8},{8,12},{12,16},{16,20},{20,24},{24,28},{28,0},{1,5},{5... | collective-permute-start | bytes 24584 | tf_op jit(solution)/shard_map/while/body/eval_jaxpr/ppermute | solution.py:23
  579.2 42.6 %collective-permute-start.2 = (bf16[256,8,128]{2,0,1:T(8,128)(2,1)S(1)}, bf16[256,8,128]{2,0,1:T(8,128)(2,1)S(1)}, u32[]{:S(2)}, u32[]{:S(2)}) collective-permute-start(bf16[256,8,128]{2,0,1:T(8,128)(2,1)S(1)} %copy.132), channel_id=1, source_target_pairs={{0,4},{4,8},{8,12},{12,16},{16,20},{20,24},{24,28},{28,0},{1,5},{5... | collective-permute-start | bytes 1572872 | tf_op jit(solution)/shard_map/while/body/eval_jaxpr/ppermute | solution.py:23
  579.2 42.6 %collective-permute-start.3 = (bf16[256,8,128]{2,0,1:T(8,128)(2,1)S(1)}, bf16[256,8,128]{2,0,1:T(8,128)(2,1)}, u32[]{:S(2)}, u32[]{:S(2)}) collective-permute-start(bf16[256,8,128]{2,0,1:T(8,128)(2,1)S(1)} %copy.133), channel_id=1, source_target_pairs={{0,4},{4,8},{8,12},{12,16},{16,20},{20,24},{24,28},{28,0},{1,5},{5... | collective-permute-start | bytes 1572872 | tf_op jit(solution)/shard_map/while/body/eval_jaxpr/ppermute | solution.py:23
  579.3 42.5 %collective-permute-start.4 = (f32[8,256]{1,0:T(8,128)S(1)}, f32[8,256]{1,0:T(8,128)S(1)}, u32[]{:S(2)}, u32[]{:S(2)}) collective-permute-start(f32[8,256]{1,0:T(8,128)S(1)} %copy.134), channel_id=1, source_target_pairs={{0,4},{4,8},{8,12},{12,16},{16,20},{20,24},{24,28},{28,0},{1,5},{5... | collective-permute-start | bytes 24584 | tf_op jit(solution)/shard_map/while/body/eval_jaxpr/ppermute | solution.py:23
  579.3 42.5 %collective-permute-start.5 = (f32[8,256]{1,0:T(8,128)S(1)}, f32[8,256]{1,0:T(8,128)S(1)}, u32[]{:S(2)}, u32[]{:S(2)}) collective-permute-start(f32[8,256]{1,0:T(8,128)S(1)} %copy.135), channel_id=1, source_target_pairs={{0,4},{4,8},{8,12},{12,16},{16,20},{20,24},{24,28},{28,0},{1,5},{5... | collective-permute-start | bytes 24584 | tf_op jit(solution)/shard_map/while/body/eval_jaxpr/ppermute | solution.py:23
  633.2 41.7 %collective-permute-start.2 = (bf16[256,8,128]{2,0,1:T(8,128)(2,1)S(1)}, bf16[256,8,128]{2,0,1:T(8,128)(2,1)S(1)}, u32[]{:S(2)}, u32[]{:S(2)}) collective-permute-start(bf16[256,8,128]{2,0,1:T(8,128)(2,1)S(1)} %copy.132), channel_id=1, source_target_pairs={{0,4},{4,8},{8,12},{12,16},{16,20},{20,24},{24,28},{28,0},{1,5},{5... | collective-permute-start | bytes 1572872 | tf_op jit(solution)/shard_map/while/body/eval_jaxpr/ppermute | solution.py:23
  633.2 41.7 %collective-permute-start.3 = (bf16[256,8,128]{2,0,1:T(8,128)(2,1)S(1)}, bf16[256,8,128]{2,0,1:T(8,128)(2,1)}, u32[]{:S(2)}, u32[]{:S(2)}) collective-permute-start(bf16[256,8,128]{2,0,1:T(8,128)(2,1)S(1)} %copy.133), channel_id=1, source_target_pairs={{0,4},{4,8},{8,12},{12,16},{16,20},{20,24},{24,28},{28,0},{1,5},{5... | collective-permute-start | bytes 1572872 | tf_op jit(solution)/shard_map/while/body/eval_jaxpr/ppermute | solution.py:23
  633.2 41.6 %collective-permute-start.4 = (f32[8,256]{1,0:T(8,128)S(1)}, f32[8,256]{1,0:T(8,128)S(1)}, u32[]{:S(2)}, u32[]{:S(2)}) collective-permute-start(f32[8,256]{1,0:T(8,128)S(1)} %copy.134), channel_id=1, source_target_pairs={{0,4},{4,8},{8,12},{12,16},{16,20},{20,24},{24,28},{28,0},{1,5},{5... | collective-permute-start | bytes 24584 | tf_op jit(solution)/shard_map/while/body/eval_jaxpr/ppermute | solution.py:23
  633.3 41.6 %collective-permute-start.5 = (f32[8,256]{1,0:T(8,128)S(1)}, f32[8,256]{1,0:T(8,128)S(1)}, u32[]{:S(2)}, u32[]{:S(2)}) collective-permute-start(f32[8,256]{1,0:T(8,128)S(1)} %copy.135), channel_id=1, source_target_pairs={{0,4},{4,8},{8,12},{12,16},{16,20},{20,24},{24,28},{28,0},{1,5},{5... | collective-permute-start | bytes 24584 | tf_op jit(solution)/shard_map/while/body/eval_jaxpr/ppermute | solution.py:23
  686.3 40.8 %collective-permute-start.2 = (bf16[256,8,128]{2,0,1:T(8,128)(2,1)S(1)}, bf16[256,8,128]{2,0,1:T(8,128)(2,1)S(1)}, u32[]{:S(2)}, u32[]{:S(2)}) collective-permute-start(bf16[256,8,128]{2,0,1:T(8,128)(2,1)S(1)} %copy.132), channel_id=1, source_target_pairs={{0,4},{4,8},{8,12},{12,16},{16,20},{20,24},{24,28},{28,0},{1,5},{5... | collective-permute-start | bytes 1572872 | tf_op jit(solution)/shard_map/while/body/eval_jaxpr/ppermute | solution.py:23
  686.3 40.8 %collective-permute-start.3 = (bf16[256,8,128]{2,0,1:T(8,128)(2,1)S(1)}, bf16[256,8,128]{2,0,1:T(8,128)(2,1)}, u32[]{:S(2)}, u32[]{:S(2)}) collective-permute-start(bf16[256,8,128]{2,0,1:T(8,128)(2,1)S(1)} %copy.133), channel_id=1, source_target_pairs={{0,4},{4,8},{8,12},{12,16},{16,20},{20,24},{24,28},{28,0},{1,5},{5... | collective-permute-start | bytes 1572872 | tf_op jit(solution)/shard_map/while/body/eval_jaxpr/ppermute | solution.py:23
  686.3 40.8 %collective-permute-start.4 = (f32[8,256]{1,0:T(8,128)S(1)}, f32[8,256]{1,0:T(8,128)S(1)}, u32[]{:S(2)}, u32[]{:S(2)}) collective-permute-start(f32[8,256]{1,0:T(8,128)S(1)} %copy.134), channel_id=1, source_target_pairs={{0,4},{4,8},{8,12},{12,16},{16,20},{20,24},{24,28},{28,0},{1,5},{5... | collective-permute-start | bytes 24584 | tf_op jit(solution)/shard_map/while/body/eval_jaxpr/ppermute | solution.py:23
  686.4 40.8 %collective-permute-start.5 = (f32[8,256]{1,0:T(8,128)S(1)}, f32[8,256]{1,0:T(8,128)S(1)}, u32[]{:S(2)}, u32[]{:S(2)}) collective-permute-start(f32[8,256]{1,0:T(8,128)S(1)} %copy.135), channel_id=1, source_target_pairs={{0,4},{4,8},{8,12},{12,16},{16,20},{20,24},{24,28},{28,0},{1,5},{5... | collective-permute-start | bytes 24584 | tf_op jit(solution)/shard_map/while/body/eval_jaxpr/ppermute | solution.py:23
  738.5 40.0 %collective-permute-start.2 = (bf16[256,8,128]{2,0,1:T(8,128)(2,1)S(1)}, bf16[256,8,128]{2,0,1:T(8,128)(2,1)S(1)}, u32[]{:S(2)}, u32[]{:S(2)}) collective-permute-start(bf16[256,8,128]{2,0,1:T(8,128)(2,1)S(1)} %copy.132), channel_id=1, source_target_pairs={{0,4},{4,8},{8,12},{12,16},{16,20},{20,24},{24,28},{28,0},{1,5},{5... | collective-permute-start | bytes 1572872 | tf_op jit(solution)/shard_map/while/body/eval_jaxpr/ppermute | solution.py:23
  738.5 40.0 %collective-permute-start.3 = (bf16[256,8,128]{2,0,1:T(8,128)(2,1)S(1)}, bf16[256,8,128]{2,0,1:T(8,128)(2,1)}, u32[]{:S(2)}, u32[]{:S(2)}) collective-permute-start(bf16[256,8,128]{2,0,1:T(8,128)(2,1)S(1)} %copy.133), channel_id=1, source_target_pairs={{0,4},{4,8},{8,12},{12,16},{16,20},{20,24},{24,28},{28,0},{1,5},{5... | collective-permute-start | bytes 1572872 | tf_op jit(solution)/shard_map/while/body/eval_jaxpr/ppermute | solution.py:23
  738.5 39.9 %collective-permute-start.4 = (f32[8,256]{1,0:T(8,128)S(1)}, f32[8,256]{1,0:T(8,128)S(1)}, u32[]{:S(2)}, u32[]{:S(2)}) collective-permute-start(f32[8,256]{1,0:T(8,128)S(1)} %copy.134), channel_id=1, source_target_pairs={{0,4},{4,8},{8,12},{12,16},{16,20},{20,24},{24,28},{28,0},{1,5},{5... | collective-permute-start | bytes 24584 | tf_op jit(solution)/shard_map/while/body/eval_jaxpr/ppermute | solution.py:23
  738.6 39.9 %collective-permute-start.5 = (f32[8,256]{1,0:T(8,128)S(1)}, f32[8,256]{1,0:T(8,128)S(1)}, u32[]{:S(2)}, u32[]{:S(2)}) collective-permute-start(f32[8,256]{1,0:T(8,128)S(1)} %copy.135), channel_id=1, source_target_pairs={{0,4},{4,8},{8,12},{12,16},{16,20},{20,24},{24,28},{28,0},{1,5},{5... | collective-permute-start | bytes 24584 | tf_op jit(solution)/shard_map/while/body/eval_jaxpr/ppermute | solution.py:23
  789.9 39.2 %collective-permute-start.2 = (bf16[256,8,128]{2,0,1:T(8,128)(2,1)S(1)}, bf16[256,8,128]{2,0,1:T(8,128)(2,1)S(1)}, u32[]{:S(2)}, u32[]{:S(2)}) collective-permute-start(bf16[256,8,128]{2,0,1:T(8,128)(2,1)S(1)} %copy.132), channel_id=1, source_target_pairs={{0,4},{4,8},{8,12},{12,16},{16,20},{20,24},{24,28},{28,0},{1,5},{5... | collective-permute-start | bytes 1572872 | tf_op jit(solution)/shard_map/while/body/eval_jaxpr/ppermute | solution.py:23
  789.9 39.2 %collective-permute-start.3 = (bf16[256,8,128]{2,0,1:T(8,128)(2,1)S(1)}, bf16[256,8,128]{2,0,1:T(8,128)(2,1)}, u32[]{:S(2)}, u32[]{:S(2)}) collective-permute-start(bf16[256,8,128]{2,0,1:T(8,128)(2,1)S(1)} %copy.133), channel_id=1, source_target_pairs={{0,4},{4,8},{8,12},{12,16},{16,20},{20,24},{24,28},{28,0},{1,5},{5... | collective-permute-start | bytes 1572872 | tf_op jit(solution)/shard_map/while/body/eval_jaxpr/ppermute | solution.py:23
  789.9 39.1 %collective-permute-start.4 = (f32[8,256]{1,0:T(8,128)S(1)}, f32[8,256]{1,0:T(8,128)S(1)}, u32[]{:S(2)}, u32[]{:S(2)}) collective-permute-start(f32[8,256]{1,0:T(8,128)S(1)} %copy.134), channel_id=1, source_target_pairs={{0,4},{4,8},{8,12},{12,16},{16,20},{20,24},{24,28},{28,0},{1,5},{5... | collective-permute-start | bytes 24584 | tf_op jit(solution)/shard_map/while/body/eval_jaxpr/ppermute | solution.py:23
  790.0 39.2 %collective-permute-start.5 = (f32[8,256]{1,0:T(8,128)S(1)}, f32[8,256]{1,0:T(8,128)S(1)}, u32[]{:S(2)}, u32[]{:S(2)}) collective-permute-start(f32[8,256]{1,0:T(8,128)S(1)} %copy.135), channel_id=1, source_target_pairs={{0,4},{4,8},{8,12},{12,16},{16,20},{20,24},{24,28},{28,0},{1,5},{5... | collective-permute-start | bytes 24584 | tf_op jit(solution)/shard_map/while/body/eval_jaxpr/ppermute | solution.py:23
  840.5 38.5 %collective-permute-start.3 = (bf16[256,8,128]{2,0,1:T(8,128)(2,1)S(1)}, bf16[256,8,128]{2,0,1:T(8,128)(2,1)}, u32[]{:S(2)}, u32[]{:S(2)}) collective-permute-start(bf16[256,8,128]{2,0,1:T(8,128)(2,1)S(1)} %copy.133), channel_id=1, source_target_pairs={{0,4},{4,8},{8,12},{12,16},{16,20},{20,24},{24,28},{28,0},{1,5},{5... | collective-permute-start | bytes 1572872 | tf_op jit(solution)/shard_map/while/body/eval_jaxpr/ppermute | solution.py:23
  (81 other events, 846.9 us)
Sparse Core Ops, SparseCore 0:
  10.7 75.4 all-gather.4
  113.4 71.3 all-gather.2
  225.3 42.9 reduce-scatter.1
where the time goes:
time: 898 us; the launch traced here: 890 us
  waiting for transfers between devices  568 us (63%)
  matrix products  142 us (16%)
  local copies, waits for them, and re-layouts  75 us (8%)
  loops' own time  40.6 us (5%)
  other arithmetic  31.7 us (4%)
  between operations  27.4 us (3%)
    ppermute x54, waiting for transfers between devices, passed_along(): return lax.ppermute(value, axis, pairs)  428 us
    all_gather x1, waiting for transfers between devices, per_device(): lax.all_gather(product_dq, 'seq', axis=0, tiled=True)  55.4 us
    all_gather x1, waiting for transfers between devices, per_device(): lax.all_gather(product_kv, 'seq', axis=0, tiled=True)  53.4 us
    dot_general x4, matrix products, apply_groups(): jnp.einsum('gts,sgk->tgk', toeplitz, grouped, precision=lax.Precision.HIG...  46.8 us
    reduce_scatter x1, waiting for transfers between devices, per_device(): lax.psum_scatter(jnp.einsum('mic,mtc->it', proj_weight, stacked, preferre...  30.4 us
    while x54, local copies, waits for them, and re-layouts  29.6 us
    cond x88, local copies, waits for them, and re-layouts  23.8 us
    another operation x1, loops' own time, per_device(): lax.fori_loop(0, seq_count, query_turn, (query_heads, grad_heads, log_nor...  21 us
  transfers between devices with their start and end apart: 57, of which 41 were waited for; matrix products, arithmetic and copies ran while one was open for 10% of the time, Pallas kernels for 0%

commit v1 on v0

--- a/solution.py
+++ b/solution.py
@@ -1,6 +1,10 @@
+import functools
+
 import jax
 import jax.numpy as jnp
 from jax import lax
+from jax.experimental import pallas as pl
+from jax.experimental.pallas import tpu as pltpu
 from jax.sharding import PartitionSpec as P
 
 HD = 128
@@ -27,7 +31,7 @@
     return current
 
 
-def per_device(
+def ring_device(
     block_order, queries, keys, values, hyena_q, hyena_k, hyena_v, hyena_grad, filters, proj_weight
 ):
     seq_count = lax.axis_size("seq")
@@ -236,6 +240,312 @@
     return (input_grad, query_grad, key_grad, value_grad)
 
 
+MESH = pl.DeviceIdType.MESH
+VMEM_SPEC = pl.BlockSpec(memory_space=pltpu.VMEM)
+SMEM_SPEC = pl.BlockSpec(memory_space=pltpu.SMEM)
+
+
+def aligned(index, size):
+    return pl.ds(pl.multiple_of(index * size, size), size)
+
+
+def greet(me, n):
+    barrier = pltpu.get_barrier_semaphore()
+    for step in range(1, n):
+        pl.semaphore_signal(
+            barrier, inc=1, device_id={"seq": lax.rem(me + step, n)}, device_id_type=MESH
+        )
+    pl.semaphore_wait(barrier, n - 1)
+
+
+def exchange(n, me, rows, send_sem, recv_sem, own_sem):
+    def parts(to_columns, src, dst, peer):
+        if to_columns:
+            return src.at[:, aligned(peer, HD)], dst.at[aligned(me, rows), :]
+        return src.at[aligned(peer, rows), :], dst.at[:, aligned(me, HD)]
+
+    def remote(tensor, to_columns, src, dst, step):
+        peer = lax.rem(me + step, n)
+        part, place = parts(to_columns, src, dst, peer)
+        return pltpu.make_async_remote_copy(
+            src_ref=part,
+            dst_ref=place,
+            send_sem=send_sem.at[tensor, step],
+            recv_sem=recv_sem.at[tensor, step],
+            device_id={"seq": peer},
+            device_id_type=MESH,
+        )
+
+    def own(tensor, to_columns, src, dst):
+        part, place = parts(to_columns, src, dst, me)
+        return pltpu.make_async_copy(part, place, own_sem.at[tensor])
+
+    def start(tensor, to_columns, src, dst):
+        for step in range(1, n):
+            remote(tensor, to_columns, src, dst, step).start()
+        own(tensor, to_columns, src, dst).start()
+
+    def wait(tensor, to_columns, src, dst):
+        for step in range(1, n):
+            remote(tensor, to_columns, src, dst, step).wait()
+        own(tensor, to_columns, src, dst).wait()
+
+    return remote, own, start, wait
+
+
+def exchange_sems(tensors, n):
+    return [
+        pltpu.SemaphoreType.DMA((tensors, n)),
+        pltpu.SemaphoreType.DMA((tensors, n)),
+        pltpu.SemaphoreType.DMA((tensors,)),
+    ]
+
+
+def move_kernel(n, to_columns, count, *refs):
+    sources, targets = refs[:count], refs[count : 2 * count]
+    me = lax.axis_index("seq")
+    rows = sources[0].shape[0] if to_columns else targets[0].shape[0]
+    _, _, start, wait = exchange(n, me, rows, *refs[2 * count :])
+    greet(me, n)
+    for t in range(count):
+        start(t, to_columns, sources[t], targets[t])
+    for t in range(count):
+        wait(t, to_columns, sources[t], targets[t])
+
+
+def move(n, to_columns, arrays, collective_id):
+    rows, columns = arrays[0].shape
+    shape = (rows * n, columns // n) if to_columns else (rows // n, columns * n)
+    count = len(arrays)
+    return pl.pallas_call(
+        functools.partial(move_kernel, n, to_columns, count),
+        out_shape=[jax.ShapeDtypeStruct(shape, a.dtype) for a in arrays],
+        in_specs=[VMEM_SPEC] * count,
+        out_specs=[VMEM_SPEC] * count,
+        scratch_shapes=exchange_sems(count, n),
+        compiler_params=pltpu.CompilerParams(
+            collective_id=collective_id, has_side_effects=True
+        ),
+    )(*arrays)
+
+
+def hyena_kernel(
+    n, groups, before_ref, after_ref, z_ref, dc_ref, causal_ref, anti_ref, q_ref, k_ref, v_ref,
+    conv_ref, dz_ref, qc_ref, kc_ref, vc_ref,
+    zc, dcc, convc, dzc, causal_high, causal_low, anti_high, anti_low, send_sem, recv_sem, own_sem,
+):
+    me = lax.axis_index("seq")
+    rows = z_ref.shape[0]
+    blocks = zc.shape[0] // BLOCK
+    remote, own, start, wait = exchange(n, me, rows, send_sem, recv_sem, own_sem)
+    greet(me, n)
+    start(0, True, z_ref, zc)
+    start(1, True, dc_ref, dcc)
+
+    window = 2 * BLOCK
+    for base_ref, high, low in (
+        (causal_ref, causal_high, causal_low), (anti_ref, anti_high, anti_low)
+    ):
+        for g in range(groups):
+            base = jnp.broadcast_to(base_ref[g : g + 1, :], (BLOCK, window))
+            table = pltpu.roll(base, 0, 1, stride=1, stride_axis=0)
+            top = table.astype(jnp.bfloat16)
+            high[:, g * window : (g + 1) * window] = top
+            low[:, g * window : (g + 1) * window] = (table - top.astype(jnp.float32)).astype(
+                jnp.bfloat16
+            )
+
+    lane_group = lax.broadcasted_iota(jnp.int32, (window, 2 * HD), 1) % HD // GROUP
+
+    def filtered(source, neighbours, high, low, target, place, own_first):
+        halves = []
+        for half in range(2):
+            block = place * 2 + half
+            own_rows = source[aligned(block, BLOCK), :]
+            picks = neighbours[aligned(block, blocks), :]
+            other = source[:BLOCK, :] * picks[0:1, :]
+            for b in range(1, blocks):
+                other = other + source[b * BLOCK : (b + 1) * BLOCK, :] * picks[b : b + 1, :]
+            pair = [own_rows, other] if own_first else [other, own_rows]
+            halves.append(jnp.concatenate(pair, axis=0))
+        wide = jnp.concatenate(halves, axis=1)
+        stack = jnp.concatenate(
+            [jnp.where(lane_group == g, wide, jnp.zeros_like(wide)) for g in range(groups)], axis=0
+        )
+        result = jnp.dot(high[...], stack, preferred_element_type=jnp.float32)
+        result = result + jnp.dot(low[...], stack, preferred_element_type=jnp.float32)
+        result = result.astype(target.dtype)
+        target[aligned(place, rows), :] = jnp.concatenate(
+            [result[:, :HD], result[:, HD:]], axis=0
+        )
+
+    def send_back(tensor, source, neighbours, high, low, target, out, own_first):
+        def one(step, carry):
+            filtered(source, neighbours, high, low, target, lax.rem(me + step, n), own_first)
+            remote(tensor, False, target, out, step).start()
+            return carry
+
+        lax.fori_loop(1, n, one, 0)
+        filtered(source, neighbours, high, low, target, me, own_first)
+        own(tensor, False, target, out).start()
+
+    wait(0, True, z_ref, zc)
+    send_back(2, zc, before_ref, causal_high, causal_low, convc, conv_ref, False)
+    wait(1, True, dc_ref, dcc)
+    send_back(3, dcc, after_ref, anti_high, anti_low, dzc, dz_ref, True)
+    attention = ((4, q_ref, qc_ref), (5, k_ref, kc_ref), (6, v_ref, vc_ref))
+    for t, src, dst in attention:
+        start(t, True, src, dst)
+    wait(2, False, convc, conv_ref)
+    wait(3, False, dzc, dz_ref)
+    for t, src, dst in attention:
+        wait(t, True, src, dst)
+
+
+def hyena(n, before, after, z, dc, causal_base, anti_base, queries, keys, values):
+    rows, columns = z.shape
+    groups = causal_base.shape[0]
+    like = jax.ShapeDtypeStruct(z.shape, jnp.bfloat16)
+    moved = jax.ShapeDtypeStruct((rows * n, HD), jnp.bfloat16)
+    table = pltpu.VMEM((BLOCK, groups * 2 * BLOCK), jnp.bfloat16)
+    return pl.pallas_call(
+        functools.partial(hyena_kernel, n, groups),
+        out_shape=[like, like, moved, moved, moved],
+        in_specs=[VMEM_SPEC] * 9,
+        out_specs=[VMEM_SPEC] * 5,
+        scratch_shapes=[pltpu.VMEM((rows * n, HD), jnp.bfloat16)] * 4
+        + [table] * 4
+        + exchange_sems(7, n),
+        compiler_params=pltpu.CompilerParams(collective_id=0, has_side_effects=True),
+    )(before, after, z, dc, causal_base, anti_base, queries, keys, values)
+
+
+def attention_kernel(
+    order_ref, holder_ref, q_ref, k_ref, v_ref, g_ref, dq_ref, dk_ref, dv_ref,
+    ks, vs, kst, dq_sum, dk_sum, dv_sum,
+):
+    blocks = order_ref.shape[0]
+    scale = HD ** (-0.5)
+    tile = 2 * BLOCK
+    for b in range(blocks):
+        at = aligned(holder_ref[b], BLOCK)
+        here = slice(b * BLOCK, (b + 1) * BLOCK)
+        rows = k_ref[at, :]
+        ks[here, :] = rows
+        kst[:, here] = rows.T
+        vs[here, :] = v_ref[at, :]
+    contract_last = (((1,), (1,)), ((), ()))
+    for i in reversed(range(blocks // 2)):
+        width = (i + 1) * tile
+        first = aligned(holder_ref[2 * i], BLOCK)
+        second = aligned(holder_ref[2 * i + 1], BLOCK)
+        q = jnp.concatenate([q_ref[first, :], q_ref[second, :]], axis=0)
+        g = jnp.concatenate([g_ref[first, :], g_ref[second, :]], axis=0)
+        scores = lax.dot_general(
+            ks[:width, :], q, contract_last, preferred_element_type=jnp.float32
+        ) * scale
+        key_at = lax.broadcasted_iota(jnp.int32, (tile, tile), 0)
+        query_at = lax.broadcasted_iota(jnp.int32, (tile, tile), 1)
+        last = jnp.where(key_at <= query_at, scores[width - tile :], -1e30)
+        if i:
+            scores = jnp.concatenate([scores[: width - tile], last], axis=0)
+        else:
+            scores = last
+        top = jnp.max(scores, axis=0, keepdims=True)
+        terms = jnp.exp(scores - top)
+        inverse = 1.0 / jnp.sum(terms, axis=0, keepdims=True)
+        prob = terms * inverse
+        prob_grad = lax.dot_general(
+            vs[:width, :], g, contract_last, preferred_element_type=jnp.float32
+        )
+        delta = jnp.sum(prob * prob_grad, axis=0, keepdims=True)
+        score_grad = (prob * (prob_grad - delta)).astype(jnp.bfloat16)
+        add_value = jnp.dot(prob.astype(jnp.bfloat16), g, preferred_element_type=jnp.float32)
+        add_key = jnp.dot(score_grad, q, preferred_element_type=jnp.float32)
+        if i == blocks // 2 - 1:
+            dv_sum[:width, :] = add_value
+            dk_sum[:width, :] = add_key
+        else:
+            dv_sum[:width, :] += add_value
+            dk_sum[:width, :] += add_key
+        query_t = jnp.dot(kst[:, :width], score_grad, preferred_element_type=jnp.float32)
+        dq_sum[i * tile : (i + 1) * tile, :] = query_t.T * scale
+    for s in range(blocks):
+        at = aligned(order_ref[s], BLOCK)
+        here = slice(s * BLOCK, (s + 1) * BLOCK)
+        dq_ref[here, :] = dq_sum[at, :].astype(dq_ref.dtype)
+        dk_ref[here, :] = (dk_sum[at, :] * scale).astype(dk_ref.dtype)
+        dv_ref[here, :] = dv_sum[at, :].astype(dv_ref.dtype)
+
+
+def attention(order, holder, q, k, v, g):
+    shape = jax.ShapeDtypeStruct(q.shape, jnp.bfloat16)
+    low = pltpu.VMEM(q.shape, jnp.bfloat16)
+    full = pltpu.VMEM(q.shape, jnp.float32)
+    return pl.pallas_call(
+        attention_kernel,
+        out_shape=[shape] * 3,
+        in_specs=[SMEM_SPEC] * 2 + [VMEM_SPEC] * 4,
+        out_specs=[VMEM_SPEC] * 3,
+        scratch_shapes=[low, low, pltpu.VMEM(q.shape[::-1], jnp.bfloat16), full, full, full],
+    )(order, holder, q, k, v, g)
+
+
+def column_device(
+    block_order, queries, keys, values, hyena_q, hyena_k, hyena_v, hyena_grad, filters, proj_weight
+):
+    n = lax.axis_size("seq")
+    me = lax.axis_index("seq")
+    blocks = block_order.shape[0]
+    ids = jnp.arange(blocks, dtype=jnp.int32)
+    holder = jnp.sum(
+        jnp.where(block_order[None, :] == ids[:, None], ids[None, :], 0), axis=1
+    ).astype(jnp.int32)
+
+    def neighbour(offset):
+        found = (block_order[None, :] == block_order[:, None] + offset).astype(jnp.bfloat16)
+        return jnp.broadcast_to(found.reshape(blocks * blocks, 1), (blocks * blocks, HD))
+
+    z = (hyena_k.astype(jnp.float32) * hyena_v.astype(jnp.float32)).astype(jnp.bfloat16)
+    dc = (hyena_grad.astype(jnp.float32) * hyena_q.astype(jnp.float32)).astype(jnp.bfloat16)
+    groups = filters.shape[0] // n
+    taps = lax.dynamic_slice_in_dim(filters, me * groups, groups, 0)
+    anti_base = jnp.pad(taps, ((0, 0), (0, KL)))
+    causal_base = jnp.pad(taps[:, ::-1], ((0, 0), (1, KL - 1)))
+    convolved, back_conv, qc, kc, vc = hyena(
+        n, neighbour(-1), neighbour(1), z, dc, causal_base, anti_base, queries, keys, values
+    )
+    convolved = convolved.astype(jnp.float32)
+    back_conv = back_conv.astype(jnp.float32)
+    stacked = jnp.stack(
+        [
+            hyena_grad.astype(jnp.float32) * convolved,
+            back_conv * hyena_v.astype(jnp.float32),
+            back_conv * hyena_k.astype(jnp.float32),
+        ]
+    ).astype(jnp.bfloat16)
+    summed = lax.psum_scatter(
+        jnp.einsum("mtc,mic->ti", stacked, proj_weight, preferred_element_type=jnp.float32),
+        "head",
+        scatter_dimension=1,
+        tiled=True,
+    )
+    input_grad = summed.astype(jnp.bfloat16)
+    (gc,) = move(n, True, [input_grad], 1)
+    grads = attention(block_order, holder, qc, kc, vc, gc)
+    query_grad, key_grad, value_grad = move(n, False, list(grads), 2)
+    return (input_grad, query_grad, key_grad, value_grad)
+
+
+def per_device(*arrays):
+    queries, filters = arrays[1], arrays[8]
+    n = lax.axis_size("seq")
+    whole_heads = queries.shape[1] == n * HD and queries.shape[0] == 2 * BLOCK
+    if whole_heads and filters.shape[0] % n == 0 and KL == BLOCK == HD:
+        return column_device(*arrays)
+    return ring_device(*arrays)
+
+
 def solution(mesh):
     placed = (
         P(),

time: 898 us -> 252 us (0.28)
  waiting for transfers between devices: 568 us -> 47.2 us
  Pallas kernels: 0 us -> 155 us
  matrix products: 142 us -> 13.8 us
  local copies, waits for them, and re-layouts: 75 us -> 9.9 us
  loops' own time: 40.6 us -> 0 us
  other arithmetic: 31.7 us -> 10.3 us
  between operations: 27.4 us -> 14.1 us
    ppermute x54 -> x0, waiting for transfers between devices: 428 us -> none  [passed_along(): return lax.ppermute(value, axis, pairs)]
    pallas_call x0 -> x4, Pallas kernels: none -> 155 us  [the longest x1 86.2 us: hyena(): pl.pallas_call(functools.partial(hyena_kernel, n, groups), out_shape=[lik...]
    dot_general x63 -> x1, matrix products: 142 us -> 13.8 us  [column_device(): jnp.einsum('mtc,mic->ti', stacked, proj_weight, preferred_element_type=jn...]
    all_gather x2 -> x0, waiting for transfers between devices: 109 us -> none  [the longest x1 55.4 us: per_device(): lax.all_gather(product_dq, 'seq', axis=0, tiled=True)]
    another operation x18 -> x0, loops' own time: 40.6 us -> none  [the longest x1 21 us: per_device(): lax.fori_loop(0, seq_count, query_turn, (query_heads, grad_heads, log_nor...]
    while x54 -> x0, local copies, waits for them, and re-layouts: 29.6 us -> none
    cond x88 -> x0, local copies, waits for them, and re-layouts: 23.8 us -> none
    reduce_scatter x1, waiting for transfers between devices: 30.4 us -> 47.2 us  [column_device(): lax.psum_scatter(jnp.einsum('mtc,mic->ti', stacked, proj_weight, preferre...]
  transfers between devices with their start and end apart: 57 -> 1, of which waited for: 41 -> 1; matrix products, arithmetic and copies ran while one was open for 10% -> 0% of each run, Pallas kernels for 0% -> 0%
where the time goes in v1:
time: 252 us; the launch traced here: 250 us
  Pallas kernels  155 us (62%)
  waiting for transfers between devices  47.2 us (19%)
  between operations  14.1 us (6%)
  matrix products  13.8 us (5%)
  other arithmetic  10.3 us (4%)
  local copies, waits for them, and re-layouts  9.9 us (4%)
    pallas_call x1, Pallas kernels, hyena(): pl.pallas_call(functools.partial(hyena_kernel, n, groups), out_shape=[lik...  86.2 us
    pallas_call x2, Pallas kernels, move(): pl.pallas_call(functools.partial(move_kernel, n, to_columns, count), out_...  55.3 us
    reduce_scatter x1, waiting for transfers between devices, column_device(): lax.psum_scatter(jnp.einsum('mtc,mic->ti', stacked, proj_weight, preferre...  47.2 us
    dot_general x1, matrix products, column_device(): jnp.einsum('mtc,mic->ti', stacked, proj_weight, preferred_element_type=jn...  13.8 us
    pallas_call x1, Pallas kernels, attention(): pl.pallas_call(attention_kernel, out_shape=[shape] * 3, in_specs=[SMEM_SP...  13.6 us
    unnamed x13, local copies, waits for them, and re-layouts  6.92 us
  transfers between devices with their start and end apart: 1, of which 1 were waited for; matrix products, arithmetic and copies ran while one was open for 0% of the time, Pallas kernels for 0%

profile of v1, /device:TPU:0, one launch (start us, length us, event | category | flops | bytes accessed | tf_op | source)
XLA Modules:
  0.0 250.4 jit_solution(1170912804948404634)
XLA Ops:
  7.2 0.0 copy-start
  7.2 0.0 copy-start.3
  7.2 0.0 copy-start.2
  7.2 0.0 copy-start.1
  7.2 0.0 reduce-scatter.2.cloned.1.call-start
  7.3 0.7 copy-done
  7.9 0.1 rev.3
  8.0 0.6 pad.9.anti_ref
  8.6 0.7 pad.8.causal_ref
  9.3 0.7 broadcast_add_fusion
  9.9 0.7 compare_convert_fusion
  10.7 0.1 reshape.49
  10.7 0.1 reshape.50
  10.8 2.2 fusion.5.dc_ref
  13.0 2.2 fusion.7.z_ref
  15.2 0.7 broadcast_in_dim.16.before_ref
  15.9 0.7 broadcast_in_dim.17.after_ref
  16.7 86.2 %shard_map.129 = (bf16[256,1024]{1,0:T(8,128)(2,1)}, bf16[256,1024]{1,0:T(8,128)(2,1)}, bf16[2048,128]{1,0:T(8,128)(2,1)}, bf16[2048,128]{1,0:T(8,128)(2,1)}, bf16[2048,128]{1,0:T(8,128)(2,1)}) custom-call(bf16[256,128]{1,0:T(8,128)(2,1)} %broadcast_in_dim.16.before_ref, bf16[256,128]{1,0:T(8,128)(2,1)} %broadcast_in_dim.17.after_ref, ...), custom_call_target="tpu_custom_call" | custom-call | tf_op jit(solution)/shard_map/pallas_call | solution.py:411
  102.9 0.0 copy-done.3
  102.9 1.8 fusion.11
  104.7 13.8 %convolution_bitcast_fusion = f32[256,4096]{1,0:T(8,128)} fusion(bf16[3,4096,1024]{2,1,0:T(8,128)(2,1)} %param.19, bf16[1,256,1024]{2,1,0:T(8,128)(2,1)S(1)} %get-tuple-element.27, bf16[1,256,1024]{2,1,0:T(8,128)(2,1)S(1)} %get-tuple-element.26, bf16[1,256,1024]{2,1,0:T(8,128)(2,1)S(1)} %get-tuple-element.32), kind=kOutput, calls=%fused_computation | convolution fusion | flops 6444023808 | bytes 30932992 | tf_op jit(solution)/shard_map/mtc,mic->ti/dot_general | solution.py:528
  118.5 0.0 reduce-scatter.2.cloned.1.call-update
  118.5 0.6 copy-done.4
  119.1 0.7 select_reduce_fusion.holder_ref
  119.8 47.2 %reduce-scatter.2.cloned.1.call-done = f32[256,1024]{1,0:T(8,128)} async-done(((f32[256,4096]{1,0:T(8,128)}), f32[256,1024]{1,0:T(8,128)}) %reduce-scatter.2.cloned.1.call-update) | async-done | bytes 1048592 | tf_op jit(solution)/shard_map/reduce_scatter | solution.py:527
  167.0 2.1 convert_element_type.67.refs_0_
  169.1 14.5 %shard_map.130.g_ref = bf16[2048,128]{1,0:T(8,128)(2,1)} custom-call(bf16[256,1024]{1,0:T(8,128)(2,1)} %convert_element_type.67.refs_0_), custom_call_target="tpu_custom_call" | custom-call | tf_op jit(solution)/shard_map/pallas_call | solution.py:320
  183.6 13.6 %shard_map.131 = (bf16[2048,128]{1,0:T(8,128)(2,1)}, bf16[2048,128]{1,0:T(8,128)(2,1)}, bf16[2048,128]{1,0:T(8,128)(2,1)}) custom-call(s32[16]{0:T(128)} %order_ref.1, s32[16]{0:T(128)} %select_reduce_fusion.holder_ref, bf16[2048,128]{1,0:T(8,128)(2,1)} %get-tuple-element.17.q_ref, bf16[2048,128]{1,0:T(8,128)(2,1)} %get-tuple-element.18.k_ref, ...), custom_call_target="tpu_custom_call" | custom-call | tf_op jit(solution)/shard_map/pallas_call | solution.py:485
  197.1 40.8 %shard_map.132 = (bf16[256,1024]{1,0:T(8,128)(2,1)}, bf16[256,1024]{1,0:T(8,128)(2,1)}, bf16[256,1024]{1,0:T(8,128)(2,1)}) custom-call(bf16[2048,128]{1,0:T(8,128)(2,1)} %get-tuple-element.20.refs_0_, bf16[2048,128]{1,0:T(8,128)(2,1)} %get-tuple-element.21.refs_1_, bf16[2048,128]{1,0:T(8,128)(2,1)} %get-tuple-element.22.refs_2_), custom_call_target="tpu_custom_call" | custom-call | tf_op jit(solution)/shard_map/pallas_call | solution.py:320
  238.0 1.9 copy.17
  239.8 1.9 copy.18
  241.7 1.9 copy.19
  (4 shorter events, 0.0 us)
Async XLA Ops:
  7.2 0.8 copy-start
  7.2 95.7 %copy-start.3 = (bf16[256,1024]{1,0:T(8,128)(2,1)S(1)}, bf16[256,1024]{1,0:T(8,128)(2,1)}, u32[]{:S(2)}) copy-start(bf16[256,1024]{1,0:T(8,128)(2,1)} %param.17) | copy-start | bytes 1572868
  7.2 95.7 %copy-start.2 = (bf16[256,1024]{1,0:T(8,128)(2,1)S(1)}, bf16[256,1024]{1,0:T(8,128)(2,1)}, u32[]{:S(2)}) copy-start(bf16[256,1024]{1,0:T(8,128)(2,1)} %param.15) | copy-start | bytes 1572868
  7.2 95.7 %copy-start.1 = (bf16[256,1024]{1,0:T(8,128)(2,1)S(1)}, bf16[256,1024]{1,0:T(8,128)(2,1)}, u32[]{:S(2)}) copy-start(bf16[256,1024]{1,0:T(8,128)(2,1)} %param.16) | copy-start | bytes 1572868
  7.2 159.8 %reduce-scatter.2.cloned.1.call-start = ((), (), s32[]{:S(2)}) async-start(), calls=%async_computation.1 | async-start | bytes 5242880 | tf_op jit(solution)/shard_map/reduce_scatter | solution.py:527
  118.5 0.7 copy-start.4
Sparse Core Ops, SparseCore 0:
  118.6 48.3 reduce-scatter.1

commit v2 on v1

--- a/solution.py
+++ b/solution.py
@@ -249,13 +249,15 @@
     return pl.ds(pl.multiple_of(index * size, size), size)
 
 
-def greet(me, n):
+def greet(me, n, head_peers=()):
     barrier = pltpu.get_barrier_semaphore()
     for step in range(1, n):
         pl.semaphore_signal(
             barrier, inc=1, device_id={"seq": lax.rem(me + step, n)}, device_id_type=MESH
         )
-    pl.semaphore_wait(barrier, n - 1)
+    for peer in head_peers:
+        pl.semaphore_signal(barrier, inc=1, device_id={"head": peer}, device_id_type=MESH)
+    pl.semaphore_wait(barrier, n - 1 + len(head_peers))
 
 
 def exchange(n, me, rows, send_sem, recv_sem, own_sem):
@@ -330,15 +332,41 @@
 
 
 def hyena_kernel(
-    n, groups, before_ref, after_ref, z_ref, dc_ref, causal_ref, anti_ref, q_ref, k_ref, v_ref,
-    conv_ref, dz_ref, qc_ref, kc_ref, vc_ref,
-    zc, dcc, convc, dzc, causal_high, causal_low, anti_high, anti_low, send_sem, recv_sem, own_sem,
+    n, heads, groups,
+    before_ref, after_ref, hq_ref, hk_ref, hv_ref, hg_ref, causal_ref, anti_ref,
+    q_ref, k_ref, v_ref, weight_ref,
+    grad_ref, qc_ref, kc_ref, vc_ref, gc_ref,
+    z_ref, dc_ref, conv_ref, dz_ref, zc, dcc, convc, dzc,
+    causal_high, causal_low, anti_high, anti_low,
+    stacked, weights, kept, pair_out, pair_in, line_out, line_in,
+    send_sem, recv_sem, own_sem, weight_sem, pair_sem, line_sem,
 ):
     me = lax.axis_index("seq")
-    rows = z_ref.shape[0]
+    head = lax.axis_index("head")
+    rows, columns = z_ref.shape
     blocks = zc.shape[0] // BLOCK
+    chips = heads // 2
+    chip, core = head // 2, lax.rem(head, 2)
+    partner = chip * 2 + 1 - core
+    along = [lax.rem(chip + step, chips) for step in range(chips)]
+    order = list(range(1, chips)) + [0]
     remote, own, start, wait = exchange(n, me, rows, send_sem, recv_sem, own_sem)
-    greet(me, n)
+
+    def weight_copy(slot, goal, m):
+        return pltpu.make_async_copy(
+            weight_ref.at[m, aligned(goal, columns), :], weights.at[slot, m],
+            weight_sem.at[slot, m],
+        )
+
+    for step in order:
+        for mine in range(2):
+            goal = along[step] * 2 + (core if mine else 1 - core)
+            for m in range(3):
+                weight_copy(2 * step + mine, goal, m).start()
+    wide_of = lambda ref: ref[...].astype(jnp.float32)
+    z_ref[...] = (wide_of(hk_ref) * wide_of(hv_ref)).astype(jnp.bfloat16)
+    dc_ref[...] = (wide_of(hg_ref) * wide_of(hq_ref)).astype(jnp.bfloat16)
+    greet(me, n, [partner] + [along[step] * 2 + core for step in range(1, chips)])
     start(0, True, z_ref, zc)
     start(1, True, dc_ref, dcc)
 
@@ -397,27 +425,101 @@
     for t, src, dst in attention:
         start(t, True, src, dst)
     wait(2, False, convc, conv_ref)
+    stacked[0] = (wide_of(hg_ref) * wide_of(conv_ref)).astype(jnp.bfloat16)
     wait(3, False, dzc, dz_ref)
+    stacked[1] = (wide_of(dz_ref) * wide_of(hv_ref)).astype(jnp.bfloat16)
+    stacked[2] = (wide_of(dz_ref) * wide_of(hk_ref)).astype(jnp.bfloat16)
+
+    def project(slot, goal, target):
+        for m in range(3):
+            weight_copy(slot, goal, m).wait()
+        tile = 2 * BLOCK
+
+        def one(j, carry):
+            total = None
+            for m in range(3):
+                part = lax.dot_general(
+                    stacked[m], weights[slot, m, aligned(j, tile), :],
+                    (((1,), (1,)), ((), ())), preferred_element_type=jnp.float32,
+                )
+                total = part if total is None else total + part
+            target[:, aligned(j, tile)] = total
+            return carry
+
+        lax.fori_loop(0, columns // tile, one, 0)
+
+    def pair_copy(step):
+        return pltpu.make_async_remote_copy(
+            src_ref=pair_out.at[step], dst_ref=pair_in.at[step],
+            send_sem=pair_sem.at[0, step], recv_sem=pair_sem.at[1, step],
+            device_id={"head": partner}, device_id_type=MESH,
+        )
+
+    def line_copy(step):
+        return pltpu.make_async_remote_copy(
+            src_ref=line_out.at[step - 1], dst_ref=line_in.at[step - 1],
+            send_sem=line_sem.at[0, step], recv_sem=line_sem.at[1, step],
+            device_id={"head": along[step] * 2 + core}, device_id_type=MESH,
+        )
+
+    for step in order:
+        project(2 * step, along[step] * 2 + 1 - core, pair_out.at[step])
+        pair_copy(step).start()
+        project(2 * step + 1, along[step] * 2 + core, kept)
+        pair_copy(step).wait()
+        if step:
+            line_out[step - 1] = kept[...] + pair_in[step]
+            line_copy(step).start()
+    total = kept[...] + pair_in[0]
+    for step in range(1, chips):
+        line_copy(step).wait()
+        total = total + line_in[step - 1]
+    grad_ref[...] = total.astype(grad_ref.dtype)
+    start(7, True, grad_ref, gc_ref)
     for t, src, dst in attention:
         wait(t, True, src, dst)
-
-
-def hyena(n, before, after, z, dc, causal_base, anti_base, queries, keys, values):
-    rows, columns = z.shape
+    wait(7, True, grad_ref, gc_ref)
+
+
+def hyena(
+    n, heads, before, after, hyena_q, hyena_k, hyena_v, hyena_grad, causal_base, anti_base,
+    queries, keys, values, proj_weight,
+):
+    rows, columns = queries.shape
     groups = causal_base.shape[0]
-    like = jax.ShapeDtypeStruct(z.shape, jnp.bfloat16)
+    chips = heads // 2
+    like = jax.ShapeDtypeStruct(queries.shape, jnp.bfloat16)
     moved = jax.ShapeDtypeStruct((rows * n, HD), jnp.bfloat16)
     table = pltpu.VMEM((BLOCK, groups * 2 * BLOCK), jnp.bfloat16)
+    low = pltpu.VMEM((rows, columns), jnp.bfloat16)
+    partial = lambda count: pltpu.VMEM((count, rows, columns), jnp.float32)
     return pl.pallas_call(
-        functools.partial(hyena_kernel, n, groups),
-        out_shape=[like, like, moved, moved, moved],
-        in_specs=[VMEM_SPEC] * 9,
+        functools.partial(hyena_kernel, n, heads, groups),
+        out_shape=[like] + [moved] * 4,
+        in_specs=[VMEM_SPEC] * 11 + [pl.BlockSpec(memory_space=pl.ANY)],
         out_specs=[VMEM_SPEC] * 5,
-        scratch_shapes=[pltpu.VMEM((rows * n, HD), jnp.bfloat16)] * 4
+        scratch_shapes=[low] * 4
+        + [pltpu.VMEM((rows * n, HD), jnp.bfloat16)] * 4
         + [table] * 4
-        + exchange_sems(7, n),
-        compiler_params=pltpu.CompilerParams(collective_id=0, has_side_effects=True),
-    )(before, after, z, dc, causal_base, anti_base, queries, keys, values)
+        + [
+            pltpu.VMEM((3, rows, columns), jnp.bfloat16),
+            pltpu.VMEM((heads, 3, columns, columns), jnp.bfloat16),
+            pltpu.VMEM((rows, columns), jnp.float32),
+            partial(chips), partial(chips), partial(chips - 1), partial(chips - 1),
+        ]
+        + exchange_sems(8, n)
+        + [
+            pltpu.SemaphoreType.DMA((heads, 3)),
+            pltpu.SemaphoreType.DMA((2, chips)),
+            pltpu.SemaphoreType.DMA((2, chips)),
+        ],
+        compiler_params=pltpu.CompilerParams(
+            collective_id=0, has_side_effects=True, vmem_limit_bytes=60 * 2**20
+        ),
+    )(
+        before, after, hyena_q, hyena_k, hyena_v, hyena_grad, causal_base, anti_base,
+        queries, keys, values, proj_weight,
+    )
 
 
 def attention_kernel(
@@ -506,32 +608,15 @@
         found = (block_order[None, :] == block_order[:, None] + offset).astype(jnp.bfloat16)
         return jnp.broadcast_to(found.reshape(blocks * blocks, 1), (blocks * blocks, HD))
 
-    z = (hyena_k.astype(jnp.float32) * hyena_v.astype(jnp.float32)).astype(jnp.bfloat16)
-    dc = (hyena_grad.astype(jnp.float32) * hyena_q.astype(jnp.float32)).astype(jnp.bfloat16)
     groups = filters.shape[0] // n
     taps = lax.dynamic_slice_in_dim(filters, me * groups, groups, 0)
     anti_base = jnp.pad(taps, ((0, 0), (0, KL)))
     causal_base = jnp.pad(taps[:, ::-1], ((0, 0), (1, KL - 1)))
-    convolved, back_conv, qc, kc, vc = hyena(
-        n, neighbour(-1), neighbour(1), z, dc, causal_base, anti_base, queries, keys, values
-    )
-    convolved = convolved.astype(jnp.float32)
-    back_conv = back_conv.astype(jnp.float32)
-    stacked = jnp.stack(
-        [
-            hyena_grad.astype(jnp.float32) * convolved,
-            back_conv * hyena_v.astype(jnp.float32),
-            back_conv * hyena_k.astype(jnp.float32),
-        ]
-    ).astype(jnp.bfloat16)
-    summed = lax.psum_scatter(
-        jnp.einsum("mtc,mic->ti", stacked, proj_weight, preferred_element_type=jnp.float32),
-        "head",
-        scatter_dimension=1,
-        tiled=True,
-    )
-    input_grad = summed.astype(jnp.bfloat16)
-    (gc,) = move(n, True, [input_grad], 1)
+    heads = lax.axis_size("head")
+    input_grad, qc, kc, vc, gc = hyena(
+        n, heads, neighbour(-1), neighbour(1), hyena_q, hyena_k, hyena_v, hyena_grad,
+        causal_base, anti_base, queries, keys, values, proj_weight,
+    )
     grads = attention(block_order, holder, qc, kc, vc, gc)
     query_grad, key_grad, value_grad = move(n, False, list(grads), 2)
     return (input_grad, query_grad, key_grad, value_grad)
@@ -541,7 +626,8 @@
     queries, filters = arrays[1], arrays[8]
     n = lax.axis_size("seq")
     whole_heads = queries.shape[1] == n * HD and queries.shape[0] == 2 * BLOCK
-    if whole_heads and filters.shape[0] % n == 0 and KL == BLOCK == HD:
+    paired = lax.axis_size("head") % 2 == 0 and lax.axis_size("head") > 2
+    if whole_heads and paired and filters.shape[0] % n == 0 and KL == BLOCK == HD:
         return column_device(*arrays)
     return ring_device(*arrays)
 

time: 252 us -> 183 us (0.73)
  waiting for transfers between devices: 47.2 us -> 0 us
  matrix products: 13.8 us -> 0 us
  between operations: 14.1 us -> 0.67 us
  Pallas kernels: 155 us -> 167 us
  other arithmetic: 10.3 us -> 2.74 us
    reduce_scatter x1 -> x0, waiting for transfers between devices: 47.2 us -> none  [column_device(): lax.psum_scatter(jnp.einsum('mtc,mic->ti', stacked, proj_weight, preferre...]
    pallas_call x1, Pallas kernels: 86.2 us -> 112 us  [hyena(): pl.pallas_call(functools.partial(hyena_kernel, n, heads, groups), out_sha...]
    pallas_call x2 -> x1, Pallas kernels: 55.3 us -> 41.5 us  [move(): pl.pallas_call(functools.partial(move_kernel, n, to_columns, count), out_...]
    dot_general x1 -> x0, matrix products: 13.8 us -> none  [column_device(): jnp.einsum('mtc,mic->ti', stacked, proj_weight, preferred_element_type=jn...]
    convert_element_type x3 -> x0, other arithmetic: 6.48 us -> none  [the longest x1 2.2 us: column_device(): (hyena_grad.astype(jnp.float32) * hyena_q.astype(jnp.float32)).astype(jnp...]
    unnamed x13 -> x6, local copies, waits for them, and re-layouts: 6.92 us -> 7.48 us
  transfers between devices with their start and end apart: 1 -> 0, of which waited for: 1 -> 0; matrix products, arithmetic and copies ran while one was open for 0% -> 0% of each run, Pallas kernels for 0% -> 0%
where the time goes in v2:
time: 183 us; the launch traced here: 181 us
  Pallas kernels  167 us (91%)
  local copies, waits for them, and re-layouts  10.5 us (6%)
  other arithmetic  2.74 us (1%)
    pallas_call x1, Pallas kernels, hyena(): pl.pallas_call(functools.partial(hyena_kernel, n, heads, groups), out_sha...  112 us
    pallas_call x1, Pallas kernels, move(): pl.pallas_call(functools.partial(move_kernel, n, to_columns, count), out_...  41.5 us
    pallas_call x1, Pallas kernels, attention(): pl.pallas_call(attention_kernel, out_shape=[shape] * 3, in_specs=[SMEM_SP...  13.6 us
    unnamed x6, local copies, waits for them, and re-layouts  7.48 us

profile of v2, /device:TPU:0, one launch (start us, length us, event | category | flops | bytes accessed | tf_op | source)
XLA Modules:
  0.0 180.9 jit_solution(5977227648861515627)
XLA Ops:
  0.6 0.0 copy-start
  0.7 1.4 select_reduce_fusion.holder_ref
  2.0 0.7 broadcast_add_fusion
  2.7 0.0 copy-done
  2.7 0.1 rev.3
  2.7 0.6 pad.9.anti_ref
  3.3 0.7 pad.8.causal_ref
  4.0 0.7 compare_convert_fusion
  4.7 0.1 reshape.50
  4.8 0.1 reshape.49
  4.9 0.7 broadcast_in_dim.16.before_ref
  5.7 0.7 broadcast_in_dim.17.after_ref
  6.4 112.0 %shard_map.129 = (bf16[256,1024]{1,0:T(8,128)(2,1)}, bf16[2048,128]{1,0:T(8,128)(2,1)}, bf16[2048,128]{1,0:T(8,128)(2,1)}, bf16[2048,128]{1,0:T(8,128)(2,1)}, bf16[2048,128]{1,0:T(8,128)(2,1)}) custom-call(bf16[256,128]{1,0:T(8,128)(2,1)} %broadcast_in_dim.16.before_ref, bf16[256,128]{1,0:T(8,128)(2,1)} %broadcast_in_dim.17.after_ref, ...), custom_call_target="tpu_custom_call" | custom-call | tf_op jit(solution)/shard_map/pallas_call | solution.py:496
  118.4 13.6 %shard_map.130 = (bf16[2048,128]{1,0:T(8,128)(2,1)}, bf16[2048,128]{1,0:T(8,128)(2,1)}, bf16[2048,128]{1,0:T(8,128)(2,1)}) custom-call(s32[16]{0:T(128)} %order_ref.1, s32[16]{0:T(128)} %select_reduce_fusion.holder_ref, bf16[2048,128]{1,0:T(8,128)(2,1)} %get-tuple-element.16.q_ref, bf16[2048,128]{1,0:T(8,128)(2,1)} %get-tuple-element.17.k_ref, ...), custom_call_target="tpu_custom_call" | custom-call | tf_op jit(solution)/shard_map/pallas_call | solution.py:587
  132.0 41.5 %shard_map.131 = (bf16[256,1024]{1,0:T(8,128)(2,1)}, bf16[256,1024]{1,0:T(8,128)(2,1)}, bf16[256,1024]{1,0:T(8,128)(2,1)}) custom-call(bf16[2048,128]{1,0:T(8,128)(2,1)} %get-tuple-element.20.refs_0_, bf16[2048,128]{1,0:T(8,128)(2,1)} %get-tuple-element.21.refs_1_, bf16[2048,128]{1,0:T(8,128)(2,1)} %get-tuple-element.22.refs_2_), custom_call_target="tpu_custom_call" | custom-call | tf_op jit(solution)/shard_map/pallas_call | solution.py:322
  173.5 1.9 %copy.18 = bf16[256,1024]{1,0:T(8,128)(2,1)} copy(bf16[256,1024]{1,0:T(8,128)(2,1)} %get-tuple-element.34) | data formatting | bytes 1048576
  175.3 1.9 %copy.19 = bf16[256,1024]{1,0:T(8,128)(2,1)} copy(bf16[256,1024]{1,0:T(8,128)(2,1)} %get-tuple-element.35) | data formatting | bytes 1048576
  177.2 1.9 %copy.20 = bf16[256,1024]{1,0:T(8,128)(2,1)} copy(bf16[256,1024]{1,0:T(8,128)(2,1)} %get-tuple-element.36) | data formatting | bytes 1048576
  179.1 1.9 %copy.21 = bf16[256,1024]{1,0:T(8,128)(2,1)} copy(bf16[256,1024]{1,0:T(8,128)(2,1)} %get-tuple-element.37) | data formatting | bytes 1048576
  (1 shorter events, 0.0 us)
Async XLA Ops:
  0.6 2.0 %copy-start = (f32[64,128]{1,0:T(8,128)S(1)}, f32[64,128]{1,0:T(8,128)}, u32[]{:S(2)}) copy-start(f32[64,128]{1,0:T(8,128)} %param.18) | copy-start | bytes 98308

commit v3 on v2

--- a/solution.py
+++ b/solution.py
@@ -249,7 +249,7 @@
     return pl.ds(pl.multiple_of(index * size, size), size)
 
 
-def greet(me, n, head_peers=()):
+def signal_peers(me, n, head_peers=()):
     barrier = pltpu.get_barrier_semaphore()
     for step in range(1, n):
         pl.semaphore_signal(
@@ -257,7 +257,11 @@
         )
     for peer in head_peers:
         pl.semaphore_signal(barrier, inc=1, device_id={"head": peer}, device_id_type=MESH)
-    pl.semaphore_wait(barrier, n - 1 + len(head_peers))
+
+
+def greet(me, n, head_peers=()):
+    signal_peers(me, n, head_peers)
+    pl.semaphore_wait(pltpu.get_barrier_semaphore(), n - 1 + len(head_peers))
 
 
 def exchange(n, me, rows, send_sem, recv_sem, own_sem):
@@ -303,37 +307,9 @@
     ]
 
 
-def move_kernel(n, to_columns, count, *refs):
-    sources, targets = refs[:count], refs[count : 2 * count]
-    me = lax.axis_index("seq")
-    rows = sources[0].shape[0] if to_columns else targets[0].shape[0]
-    _, _, start, wait = exchange(n, me, rows, *refs[2 * count :])
-    greet(me, n)
-    for t in range(count):
-        start(t, to_columns, sources[t], targets[t])
-    for t in range(count):
-        wait(t, to_columns, sources[t], targets[t])
-
-
-def move(n, to_columns, arrays, collective_id):
-    rows, columns = arrays[0].shape
-    shape = (rows * n, columns // n) if to_columns else (rows // n, columns * n)
-    count = len(arrays)
-    return pl.pallas_call(
-        functools.partial(move_kernel, n, to_columns, count),
-        out_shape=[jax.ShapeDtypeStruct(shape, a.dtype) for a in arrays],
-        in_specs=[VMEM_SPEC] * count,
-        out_specs=[VMEM_SPEC] * count,
-        scratch_shapes=exchange_sems(count, n),
-        compiler_params=pltpu.CompilerParams(
-            collective_id=collective_id, has_side_effects=True
-        ),
-    )(*arrays)
-
-
 def hyena_kernel(
     n, heads, groups,
-    before_ref, after_ref, hq_ref, hk_ref, hv_ref, hg_ref, causal_ref, anti_ref,
+    picks_ref, hq_ref, hk_ref, hv_ref, hg_ref, base_ref,
     q_ref, k_ref, v_ref, weight_ref,
     grad_ref, qc_ref, kc_ref, vc_ref, gc_ref,
     z_ref, dc_ref, conv_ref, dz_ref, zc, dcc, convc, dzc,
@@ -371,11 +347,11 @@
     start(1, True, dc_ref, dcc)
 
     window = 2 * BLOCK
-    for base_ref, high, low in (
-        (causal_ref, causal_high, causal_low), (anti_ref, anti_high, anti_low)
-    ):
+    before_ref = picks_ref.at[: blocks * blocks, :]
+    after_ref = picks_ref.at[blocks * blocks :, :]
+    for at, high, low in ((0, causal_high, causal_low), (groups, anti_high, anti_low)):
         for g in range(groups):
-            base = jnp.broadcast_to(base_ref[g : g + 1, :], (BLOCK, window))
+            base = jnp.broadcast_to(base_ref[at + g : at + g + 1, :], (BLOCK, window))
             table = pltpu.roll(base, 0, 1, stride=1, stride_axis=0)
             top = table.astype(jnp.bfloat16)
             high[:, g * window : (g + 1) * window] = top
@@ -482,11 +458,11 @@
 
 
 def hyena(
-    n, heads, before, after, hyena_q, hyena_k, hyena_v, hyena_grad, causal_base, anti_base,
+    n, heads, picks, hyena_q, hyena_k, hyena_v, hyena_grad, bases,
     queries, keys, values, proj_weight,
 ):
     rows, columns = queries.shape
-    groups = causal_base.shape[0]
+    groups = bases.shape[0] // 2
     chips = heads // 2
     like = jax.ShapeDtypeStruct(queries.shape, jnp.bfloat16)
     moved = jax.ShapeDtypeStruct((rows * n, HD), jnp.bfloat16)
@@ -496,7 +472,7 @@
     return pl.pallas_call(
         functools.partial(hyena_kernel, n, heads, groups),
         out_shape=[like] + [moved] * 4,
-        in_specs=[VMEM_SPEC] * 11 + [pl.BlockSpec(memory_space=pl.ANY)],
+        in_specs=[VMEM_SPEC] * 9 + [pl.BlockSpec(memory_space=pl.ANY)],
         out_specs=[VMEM_SPEC] * 5,
         scratch_shapes=[low] * 4
         + [pltpu.VMEM((rows * n, HD), jnp.bfloat16)] * 4
@@ -517,80 +493,129 @@
             collective_id=0, has_side_effects=True, vmem_limit_bytes=60 * 2**20
         ),
     )(
-        before, after, hyena_q, hyena_k, hyena_v, hyena_grad, causal_base, anti_base,
+        picks, hyena_q, hyena_k, hyena_v, hyena_grad, bases,
         queries, keys, values, proj_weight,
     )
 
 
 def attention_kernel(
-    order_ref, holder_ref, q_ref, k_ref, v_ref, g_ref, dq_ref, dk_ref, dv_ref,
-    ks, vs, kst, dq_sum, dk_sum, dv_sum,
+    n, order_ref, holder_ref, q_ref, k_ref, v_ref, g_ref, dq_ref, dk_ref, dv_ref,
+    ks, vs, kst, prob, dq_sum, dk_sum, dv_sum, dq_low, dk_low, dv_low, send_sem, recv_sem, own_sem,
 ):
+    me = lax.axis_index("seq")
     blocks = order_ref.shape[0]
+    _, _, start, wait = exchange(n, me, dq_ref.shape[0], send_sem, recv_sem, own_sem)
+    signal_peers(me, n)
     scale = HD ** (-0.5)
     tile = 2 * BLOCK
+    contract_last = (((1,), (1,)), ((), ()))
     for b in range(blocks):
-        at = aligned(holder_ref[b], BLOCK)
         here = slice(b * BLOCK, (b + 1) * BLOCK)
-        rows = k_ref[at, :]
+        rows = k_ref[holder_ref[b]]
         ks[here, :] = rows
         kst[:, here] = rows.T
-        vs[here, :] = v_ref[at, :]
-    contract_last = (((1,), (1,)), ((), ()))
+        vs[here, :] = v_ref[holder_ref[b]]
+
+    def pair(ref, i):
+        return jnp.concatenate([ref[holder_ref[2 * i]], ref[holder_ref[2 * i + 1]]], axis=0)
+
+    def add(total, value, i):
+        value = value.reshape(2 * i + 2, BLOCK, HD)
+        if i == blocks // 2 - 1:
+            total[...] = value
+        else:
+            total[: 2 * i + 2] += value
+
+    def stored(i):
+        return slice(tile * i * (i + 1) // 2, tile * (i + 1) * (i + 2) // 2)
+
+    def give(total, factor, low):
+        for s in range(blocks):
+            rows = total[order_ref[s]]
+            rows = rows if factor is None else rows * factor
+            low[s * BLOCK : (s + 1) * BLOCK, :] = rows.astype(low.dtype)
+
     for i in reversed(range(blocks // 2)):
         width = (i + 1) * tile
-        first = aligned(holder_ref[2 * i], BLOCK)
-        second = aligned(holder_ref[2 * i + 1], BLOCK)
-        q = jnp.concatenate([q_ref[first, :], q_ref[second, :]], axis=0)
-        g = jnp.concatenate([g_ref[first, :], g_ref[second, :]], axis=0)
+        q = pair(q_ref, i)
         scores = lax.dot_general(
             ks[:width, :], q, contract_last, preferred_element_type=jnp.float32
         ) * scale
         key_at = lax.broadcasted_iota(jnp.int32, (tile, tile), 0)
         query_at = lax.broadcasted_iota(jnp.int32, (tile, tile), 1)
         last = jnp.where(key_at <= query_at, scores[width - tile :], -1e30)
-        if i:
-            scores = jnp.concatenate([scores[: width - tile], last], axis=0)
-        else:
-            scores = last
-        top = jnp.max(scores, axis=0, keepdims=True)
-        terms = jnp.exp(scores - top)
-        inverse = 1.0 / jnp.sum(terms, axis=0, keepdims=True)
-        prob = terms * inverse
+        scores = jnp.concatenate([scores[: width - tile], last], axis=0) if i else last
+        terms = jnp.exp(scores - jnp.max(scores, axis=0, keepdims=True))
+        chance = terms * (1.0 / jnp.sum(terms, axis=0, keepdims=True))
+        prob[stored(i), :] = chance
+        add(
+            dv_sum,
+            jnp.dot(chance.astype(jnp.bfloat16), pair(g_ref, i), preferred_element_type=jnp.float32),
+            i,
+        )
+    give(dv_sum, None, dv_low)
+    pl.semaphore_wait(pltpu.get_barrier_semaphore(), n - 1)
+    start(0, False, dv_low, dv_ref)
+    for i in reversed(range(blocks // 2)):
+        width = (i + 1) * tile
         prob_grad = lax.dot_general(
-            vs[:width, :], g, contract_last, preferred_element_type=jnp.float32
-        )
-        delta = jnp.sum(prob * prob_grad, axis=0, keepdims=True)
-        score_grad = (prob * (prob_grad - delta)).astype(jnp.bfloat16)
-        add_value = jnp.dot(prob.astype(jnp.bfloat16), g, preferred_element_type=jnp.float32)
-        add_key = jnp.dot(score_grad, q, preferred_element_type=jnp.float32)
-        if i == blocks // 2 - 1:
-            dv_sum[:width, :] = add_value
-            dk_sum[:width, :] = add_key
-        else:
-            dv_sum[:width, :] += add_value
-            dk_sum[:width, :] += add_key
+            vs[:width, :], pair(g_ref, i), contract_last, preferred_element_type=jnp.float32
+        )
+        chance = prob[stored(i), :]
+        delta = jnp.sum(chance * prob_grad, axis=0, keepdims=True)
+        score_grad = (chance * (prob_grad - delta)).astype(jnp.bfloat16)
+        add(
+            dk_sum,
+            jnp.dot(score_grad, pair(q_ref, i), preferred_element_type=jnp.float32),
+            i,
+        )
         query_t = jnp.dot(kst[:, :width], score_grad, preferred_element_type=jnp.float32)
-        dq_sum[i * tile : (i + 1) * tile, :] = query_t.T * scale
-    for s in range(blocks):
-        at = aligned(order_ref[s], BLOCK)
-        here = slice(s * BLOCK, (s + 1) * BLOCK)
-        dq_ref[here, :] = dq_sum[at, :].astype(dq_ref.dtype)
-        dk_ref[here, :] = (dk_sum[at, :] * scale).astype(dk_ref.dtype)
-        dv_ref[here, :] = dv_sum[at, :].astype(dv_ref.dtype)
-
-
-def attention(order, holder, q, k, v, g):
-    shape = jax.ShapeDtypeStruct(q.shape, jnp.bfloat16)
-    low = pltpu.VMEM(q.shape, jnp.bfloat16)
-    full = pltpu.VMEM(q.shape, jnp.float32)
+        dq_sum[2 * i : 2 * i + 2] = (query_t.T * scale).reshape(2, BLOCK, HD)
+    give(dq_sum, None, dq_low)
+    start(1, False, dq_low, dq_ref)
+    give(dk_sum, scale, dk_low)
+    start(2, False, dk_low, dk_ref)
+    wait(0, False, dv_low, dv_ref)
+    wait(1, False, dq_low, dq_ref)
+    wait(2, False, dk_low, dk_ref)
+
+
+def attention(n, order, holder, *tensors):
+    rows = tensors[0].shape[0]
+    blocks = rows // BLOCK
+    low = pltpu.VMEM((rows, HD), jnp.bfloat16)
+    full = pltpu.VMEM((blocks, BLOCK, HD), jnp.float32)
+    tiles = rows // (2 * BLOCK)
+    stored = 2 * BLOCK * tiles * (tiles + 1) // 2
     return pl.pallas_call(
-        attention_kernel,
-        out_shape=[shape] * 3,
+        functools.partial(attention_kernel, n),
+        out_shape=[jax.ShapeDtypeStruct((rows // n, HD * n), jnp.bfloat16)] * 3,
         in_specs=[SMEM_SPEC] * 2 + [VMEM_SPEC] * 4,
         out_specs=[VMEM_SPEC] * 3,
-        scratch_shapes=[low, low, pltpu.VMEM(q.shape[::-1], jnp.bfloat16), full, full, full],
-    )(order, holder, q, k, v, g)
+        scratch_shapes=[low, low, pltpu.VMEM((HD, rows), jnp.bfloat16)]
+        + [pltpu.VMEM((stored, 2 * BLOCK), jnp.float32)]
+        + [full] * 3
+        + [low] * 3
+        + exchange_sems(3, n),
+        compiler_params=pltpu.CompilerParams(
+            collective_id=1, has_side_effects=True, vmem_limit_bytes=50 * 2**20
+        ),
+    )(order, holder, *[t.reshape(blocks, BLOCK, HD) for t in tensors])
+
+
+def land_kernel(count, *refs):
+    for source, target in zip(refs[:count], refs[count:]):
+        target[...] = source[...]
+
+
+def land(*arrays):
+    count = len(arrays)
+    return pl.pallas_call(
+        functools.partial(land_kernel, count),
+        out_shape=[jax.ShapeDtypeStruct(a.shape, a.dtype) for a in arrays],
+        in_specs=[VMEM_SPEC] * count,
+        out_specs=[VMEM_SPEC] * count,
+    )(*arrays)
 
 
 def column_device(
@@ -604,22 +629,26 @@
         jnp.where(block_order[None, :] == ids[:, None], ids[None, :], 0), axis=1
     ).astype(jnp.int32)
 
-    def neighbour(offset):
-        found = (block_order[None, :] == block_order[:, None] + offset).astype(jnp.bfloat16)
-        return jnp.broadcast_to(found.reshape(blocks * blocks, 1), (blocks * blocks, HD))
-
+    wanted = jnp.concatenate([block_order - 1, block_order + 1])
+    found = wanted[:, None, None] == block_order[None, :, None]
+    picks = jnp.broadcast_to(found, (2 * blocks, blocks, HD)).astype(jnp.bfloat16)
+    picks = picks.reshape(2 * blocks * blocks, HD)
     groups = filters.shape[0] // n
     taps = lax.dynamic_slice_in_dim(filters, me * groups, groups, 0)
-    anti_base = jnp.pad(taps, ((0, 0), (0, KL)))
-    causal_base = jnp.pad(taps[:, ::-1], ((0, 0), (1, KL - 1)))
+    gap = jnp.zeros((groups, 1), taps.dtype)
+    bases = jnp.concatenate(
+        [
+            jnp.concatenate([gap, taps[:, ::-1], jnp.zeros((groups, KL - 1), taps.dtype)], axis=1),
+            jnp.concatenate([taps, jnp.zeros_like(taps)], axis=1),
+        ],
+        axis=0,
+    )
     heads = lax.axis_size("head")
     input_grad, qc, kc, vc, gc = hyena(
-        n, heads, neighbour(-1), neighbour(1), hyena_q, hyena_k, hyena_v, hyena_grad,
-        causal_base, anti_base, queries, keys, values, proj_weight,
-    )
-    grads = attention(block_order, holder, qc, kc, vc, gc)
-    query_grad, key_grad, value_grad = move(n, False, list(grads), 2)
-    return (input_grad, query_grad, key_grad, value_grad)
+        n, heads, picks, hyena_q, hyena_k, hyena_v, hyena_grad, bases, queries, keys, values, proj_weight,
+    )
+    grads = attention(n, block_order, holder, qc, kc, vc, gc)
+    return tuple(land(input_grad, *grads))
 
 
 def per_device(*arrays):

time: 183 us -> 170 us (0.929)
  Pallas kernels: 167 us -> 158 us
  local copies, waits for them, and re-layouts: 10.5 us -> 8.32 us
    pallas_call x2, Pallas kernels: 55 us -> 46.1 us  [the longest x1 43.3 us: attention(): pl.pallas_call(functools.partial(attention_kernel, n), out_shape=[jax.Sha...]
    unnamed x6 -> x18, local copies, waits for them, and re-layouts: 7.48 us -> 6.55 us
where the time goes in v3:
time: 170 us; the launch traced here: 169 us
  Pallas kernels  158 us (93%)
  local copies, waits for them, and re-layouts  8.32 us (5%)
  other arithmetic  2.25 us (1%)
    pallas_call x1, Pallas kernels, hyena(): pl.pallas_call(functools.partial(hyena_kernel, n, heads, groups), out_sha...  112 us
    pallas_call x1, Pallas kernels, attention(): pl.pallas_call(functools.partial(attention_kernel, n), out_shape=[jax.Sha...  43.3 us
    unnamed x18, local copies, waits for them, and re-layouts  6.55 us

profile of v3, /device:TPU:0, one launch (start us, length us, event | category | flops | bytes accessed | tf_op | source)
XLA Modules:
  0.0 169.4 jit_solution(11576503665033740658)
XLA Ops:
  0.6 0.0 copy-start
  0.6 0.0 copy-start.8
  0.7 0.8 select_reduce_fusion.holder_ref
  1.5 0.7 broadcast_add_fusion.1
  2.2 0.1 pad_add_fusion
  2.2 0.0 copy-done
  2.2 0.1 rev.3
  2.3 0.7 select_maximum_fusion.base_ref
  3.0 0.1 eq.36
  3.1 0.1 eq.37
  3.1 0.7 eq.38
  3.8 0.1 eq.39
  3.9 0.8 broadcast_in_dim.16.picks_ref
  4.7 112.0 %shard_map.129 = (bf16[256,1024]{1,0:T(8,128)(2,1)}, bf16[2048,128]{1,0:T(8,128)(2,1)}, bf16[2048,128]{1,0:T(8,128)(2,1)}, bf16[2048,128]{1,0:T(8,128)(2,1)}, bf16[2048,128]{1,0:T(8,128)(2,1)}) custom-call(bf16[512,128]{1,0:T(8,128)(2,1)} %broadcast_in_dim.16.picks_ref, bf16[256,1024]{1,0:T(8,128)(2,1)} %hq_ref.1, bf16[256,1024]{1,0:T(8,128)(2,1)} %hk_ref.1, ...), custom_call_target="tpu_custom_call" | custom-call | tf_op jit(solution)/shard_map/pallas_call | solution.py:472
  116.7 0.0 copy-done.8
  116.7 0.0 copy-start.4
  116.7 1.0 copy-done.4
  117.8 0.0 copy-start.5
  117.8 1.0 copy-done.5
  118.8 0.0 copy-start.6
  118.8 1.0 copy-done.6
  119.8 0.0 copy-start.7
  119.8 1.0 copy-done.7
  120.9 43.3 %shard_map.130 = (bf16[256,1024]{1,0:T(8,128)(2,1)S(1)}, bf16[256,1024]{1,0:T(8,128)(2,1)S(1)}, bf16[256,1024]{1,0:T(8,128)(2,1)S(1)}) custom-call(s32[16]{0:T(128)S(1)} %copy-done.8, s32[16]{0:T(128)S(1)} %select_reduce_fusion.holder_ref, bf16[16,128,128]{2,1,0:T(8,128)(2,1)S(1)} %bitcast.6, bf16[16,128,128]{2,1,0:T(8,128)(2,1)S(1)} %bitcast.7, ...), custom_call_target="tpu_custom_call" | custom-call | tf_op jit(solution)/shard_map/pallas_call | solution.py:590
  164.2 0.0 copy-start.1
  164.2 0.8 copy-done.1
  164.9 0.0 copy-start.2
  164.9 0.8 copy-done.2
  165.8 0.0 copy-start.3
  165.8 0.8 copy-done.3
  166.6 2.9 %shard_map.131 = (bf16[256,1024]{1,0:T(8,128)(2,1)}, bf16[256,1024]{1,0:T(8,128)(2,1)}, bf16[256,1024]{1,0:T(8,128)(2,1)}, bf16[256,1024]{1,0:T(8,128)(2,1)}) custom-call(bf16[256,1024]{1,0:T(8,128)(2,1)} %get-tuple-element.12.refs_0_, bf16[256,1024]{1,0:T(8,128)(2,1)} %copy-done.1, bf16[256,1024]{1,0:T(8,128)(2,1)} %copy-done.2, bf16[256,1024]{1,0:T(8,128)(2,1)} %copy-done.3), custom_call_target="tpu_custom_call" | custom-call | tf_op jit(solution)/shard_map/pallas_call | solution.py:613
  (4 shorter events, 0.0 us)
Async XLA Ops:
  0.6 1.6 copy-start
  0.6 116.1 %copy-start.8 = (s32[16]{0:T(128)S(1)}, s32[16]{0:T(128)}, u32[]{:S(2)}) copy-start(s32[16]{0:T(128)} %order_ref.1) | copy-start | bytes 196
  116.7 1.0 copy-start.4
  117.8 1.0 copy-start.5
  118.8 1.0 copy-start.6
  119.8 1.0 copy-start.7
  164.2 0.8 copy-start.1
  164.9 0.8 copy-start.2
  165.8 0.8 copy-start.3
